TPU v7x, 32 devices: a whole 2x2x4 slice. The times are simulated.
32 devices in a mesh: groups: 2 (over x), att: 8 (over z, y), exp: 2 (over core).
Axes of the slice: x: 2, y: 2, z: 4, core: 2. Of those that a mesh axis runs over, the one named last changes fastest.
Arguments:
- query: bfloat16 [2048, 2048], P(('groups', 'att'), 'exp'), parts along dimension 0, may hold values from -9 to 9
- new_key: bfloat16 [2048, 256], P(('groups', 'att'), 'exp'), parts along dimension 0, may hold values from -6 to 6
- new_value: bfloat16 [2048, 256], P(('groups', 'att'), 'exp'), parts along dimension 0, may hold values from -6 to 6
- cache_keys: bfloat16 [2048, 64, 256], P(('groups', 'att'), None, 'exp'), parts along dimension 0, may hold values from -9 to 9
- cache_values: bfloat16 [2048, 64, 256], P(('groups', 'att'), None, 'exp'), parts along dimension 0, may hold values from -6 to 6
- lengths: int32 [2048], P(('groups', 'att')), parts along dimension 0, may hold values from 2 to 64, as said below
- out_proj: bfloat16 [2048, 2880], P('exp'), may hold values from -0.125 to 0.125
- residual: bfloat16 [2048, 2880], P(('groups', 'att', 'exp')), parts along dimension 0, may hold values from -6 to 6
- norm_gain: float32 [2880], replicated, may hold values from 0.25 to 1.75
- router: float32 [2880, 8], replicated, may hold values from -0.21875 to 0.21875
- routes: int32 [2048, 4], P(('groups', 'att', 'exp')), parts along dimension 0, may hold values from 0 to 7, all different within a row; in each aligned block of 64 rows (0 to 63, 64 to 127, ...) at most 64 rows name the same one
- w_gate: bfloat16 [8, 2880, 1440], P('att', None, 'exp'), may hold values from -0.109375 to 0.109375
- w_up: bfloat16 [8, 2880, 1440], P('att', None, 'exp'), may hold values from -0.109375 to 0.109375
- w_down: bfloat16 [8, 1440, 2880], P('att', 'exp'), may hold values from -0.15625 to 0.15625
Outputs:
- mixed: bfloat16 [2048, 2880], P(('groups', 'att', 'exp')), parts along dimension 0
There are 2 independent parts, one for each index of `groups`. A program takes and returns all parts, laid end to end along the dimension named above; an argument that names none is the same for every part. Nothing has to cross between parts.
Inputs may be any that keep to these rules, and one draw needn't show every extreme that they name: `routes`: each row names 4 different experts. Among the 64 rows of one device (aligned blocks in order) no expert is named more than 64 times, and that count is reached in every draw. `lengths`: every eighth request, starting with the first, uses all 64 cached positions.
All inputs are finite; a program needn't handle non-finite values.
Results may differ from a plain program's by a relative error of at most 0.0065.
Values may be sent and summed in bfloat16 or wider, within the bound.
A program may use at most 128 MiB of HBM per device.

v0:
```python
import math

import jax
import jax.numpy as jnp
from jax import lax
from jax.sharding import PartitionSpec as P

HEAD = 64


def attend(query, new_key, new_value, cache_keys, cache_values, lengths):
    requests = query.shape[0]
    cache_len = cache_keys.shape[1]
    value_heads = new_key.shape[1] // HEAD
    group_size = query.shape[1] // new_key.shape[1]
    inverse_root = 1.0 / math.sqrt(HEAD)
    queries = query.reshape(requests, value_heads, group_size, HEAD)
    cached_k = cache_keys.reshape(requests, cache_len, value_heads, HEAD)
    cached_v = cache_values.reshape(requests, cache_len, value_heads, HEAD)
    fresh_k = new_key.reshape(requests, value_heads, HEAD)
    fresh_v = new_value.astype(jnp.float32).reshape(requests, value_heads, HEAD)
    cached_scores = (
        jnp.einsum("rjgd,rljd->rjgl", queries, cached_k, preferred_element_type=jnp.float32)
        * inverse_root
    )
    fresh_scores = (
        jnp.einsum("rjgd,rjd->rjg", queries, fresh_k, preferred_element_type=jnp.float32)
        * inverse_root
    )
    live_mask = jnp.arange(cache_len)[None, :] < lengths[:, None]
    cached_scores = jnp.where(live_mask[:, None, None, :], cached_scores, -1e30)
    highest = jnp.maximum(jnp.max(cached_scores, axis=-1), fresh_scores)
    cached_exp = jnp.exp(cached_scores - highest[..., None])
    fresh_exp = jnp.exp(fresh_scores - highest)
    totals = jnp.sum(cached_exp, axis=-1) + fresh_exp
    cached_probs = (cached_exp / totals[..., None]).astype(jnp.bfloat16)
    fresh_probs = (fresh_exp / totals).astype(jnp.bfloat16)
    output = jnp.einsum(
        "rjgl,rljd->rjgd", cached_probs, cached_v, preferred_element_type=jnp.float32
    )
    output = output + fresh_probs.astype(jnp.float32)[..., None] * fresh_v[:, :, None, :]
    return output.astype(jnp.bfloat16).reshape(requests, query.shape[1])


def per_device(
    query,
    new_key,
    new_value,
    cache_keys,
    cache_values,
    lengths,
    out_proj,
    residual,
    norm_gain,
    router,
    routes,
    w_gate,
    w_up,
    w_down,
):
    attended = attend(query, new_key, new_value, cache_keys, cache_values, lengths)
    summed = lax.psum_scatter(
        jnp.dot(attended, out_proj, preferred_element_type=jnp.float32),
        "exp",
        scatter_dimension=0,
        tiled=True,
    )
    hidden_state = residual.astype(jnp.float32) + summed
    mean_square = jnp.mean(hidden_state * hidden_state, axis=-1, keepdims=True)
    normed = (hidden_state * lax.rsqrt(mean_square + 1e-05) * norm_gain).astype(jnp.bfloat16)
    logits = jnp.dot(normed.astype(jnp.float32), router, precision=lax.Precision.HIGHEST)
    chosen_logits = jnp.take_along_axis(logits, routes, axis=1)
    squashed = jax.nn.sigmoid(chosen_logits)
    gate_weights = squashed / jnp.sum(squashed, axis=1, keepdims=True)
    experts = lax.axis_size("att")
    own_rows = routes.shape[0]
    top_count = routes.shape[1]
    width = normed.shape[1]
    capacity = 2 * own_rows * top_count // experts
    flat_routes = routes.reshape(-1)
    onehot = (flat_routes[:, None] == jnp.arange(experts)[None, :]).astype(jnp.int32)
    before = jnp.cumsum(onehot, axis=0) - onehot
    slot_index = jnp.sum(before * onehot, axis=1)
    target = flat_routes * capacity + slot_index
    placing = (jnp.arange(experts * capacity)[:, None] == target[None, :]).reshape(
        experts * capacity, own_rows, top_count
    )
    placing = jnp.any(placing, axis=2).astype(jnp.bfloat16)
    outgoing = jnp.dot(placing, normed, preferred_element_type=jnp.float32).astype(jnp.bfloat16)
    outgoing = outgoing.reshape(experts, capacity, width)
    gate_matrix = w_gate[0]
    up_matrix = w_up[0]
    down_matrix = w_down[0]
    arrived = lax.all_to_all(outgoing, "att", split_axis=0, concat_axis=0, tiled=True)
    routed_block = lax.all_gather(arrived, "exp", axis=1, tiled=True)
    leading = routed_block.shape[:-1]
    flat_rows = routed_block.reshape(-1, routed_block.shape[-1])
    gate_part = jnp.dot(flat_rows, gate_matrix, preferred_element_type=jnp.float32)
    up_part = jnp.dot(flat_rows, up_matrix, preferred_element_type=jnp.float32)
    activated = (jax.nn.silu(gate_part) * up_part).astype(jnp.bfloat16)
    result = jnp.dot(activated, down_matrix, preferred_element_type=jnp.float32)
    partial_value = result.reshape(leading + (result.shape[-1],))
    partial_value = lax.optimization_barrier(partial_value.astype(jnp.bfloat16)).astype(jnp.float32)
    summed_all = lax.psum(partial_value.astype(jnp.bfloat16), "exp").astype(jnp.float32)
    own_block = lax.dynamic_slice_in_dim(summed_all, lax.axis_index("exp") * capacity, capacity, 1)
    finished = own_block.astype(jnp.bfloat16)
    returned = lax.all_to_all(finished, "att", split_axis=0, concat_axis=0, tiled=True)
    flat_back = returned.reshape(-1, returned.shape[-1])
    picked = jnp.take(flat_back, target, axis=0).astype(jnp.float32)
    picked = picked.reshape(own_rows, top_count, returned.shape[-1])
    combined = jnp.sum(picked * gate_weights[:, :, None], axis=1)
    return (hidden_state + combined).astype(jnp.bfloat16)


def solution(mesh):
    in_specs = (
        P(("groups", "att"), "exp"),
        P(("groups", "att"), "exp"),
        P(("groups", "att"), "exp"),
        P(("groups", "att"), None, "exp"),
        P(("groups", "att"), None, "exp"),
        P(("groups", "att")),
        P("exp", None),
        P(("groups", "att", "exp"), None),
        P(),
        P(),
        P(("groups", "att", "exp"), None),
        P("att", None, "exp"),
        P("att", None, "exp"),
        P("att", "exp", None),
    )
    out_specs = P(("groups", "att", "exp"), None)
    return jax.shard_map(
        per_device, mesh=mesh, in_specs=in_specs, out_specs=out_specs, check_vma=False
    )
```

profile of v0, /device:TPU:0, one launch (start us, length us, event | category | flops | bytes accessed | tf_op | source)
XLA Modules:
  0.0 298.4 jit_solution(6635247010307698709)
XLA Ops:
  6.5 3.3 %copy.118 = bf16[128,64,128]{0,2,1:T(8,128)(2,1)S(1)} copy(bf16[128,64,128]{2,1,0:T(8,128)(2,1)} %param.18) | data formatting | bytes 4194304 | tf_op args[4]
  9.9 6.5 %copy.119 = bf16[128,64,2,64]{3,1,2,0:T(8,128)(2,1)} copy(bf16[128,64,2,64]{0,3,2,1:T(8,128)(2,1)S(1)} %bitcast.61) | data formatting | bytes 4194304 | tf_op jit(solution)/shard_map/reshape | solution.py:19
  16.5 0.4 copy.111
  17.0 3.3 %copy.110 = bf16[128,64,128]{0,2,1:T(8,128)(2,1)S(1)} copy(bf16[128,64,128]{2,1,0:T(8,128)(2,1)} %param.17) | data formatting | bytes 4194304 | tf_op args[3]
  20.3 6.5 %copy.112 = bf16[128,64,2,64]{3,1,2,0:T(8,128)(2,1)} copy(bf16[128,64,2,64]{0,3,2,1:T(8,128)(2,1)S(1)} %bitcast.62) | data formatting | bytes 4194304 | tf_op jit(solution)/shard_map/reshape | solution.py:18
  27.2 4.6 %fusion.25 = (f32[128,2,8]{2,1,0:T(2,128)S(1)}, f32[128,2,8,64]{3,2,1,0:T(8,128)S(1)}) fusion(bf16[128,2,8,64]{3,2,1,0:T(8,128)(2,1)S(1)} %copy.111, bf16[128,64,2,64]{3,1,2,0:T(8,128)(2,1)} %copy.112, pred[128,64]{1,0:T(8,128)(4,1)S(1)} %iota_compare_fusion.1), kind=kOutput, calls=%fused_computation.57 | convolution fusion | flops 17168384 | bytes 2899968 | tf_op jit(solution)/shard_map/rjgd,rljd->rjgl/dot_general | solution.py:23
  32.3 0.8 fusion.14
  33.4 3.5 %fusion.13 = bf16[128,2,8,64]{3,2,1,0:T(8,128)(2,1)S(1)} fusion(bf16[128,64,2,64]{3,1,2,0:T(8,128)(2,1)} %copy.119, f32[128,2,8,64]{3,2,1,0:T(8,128)S(1)} %get-tuple-element.10, f32[128,2,64]{2,1,0:T(2,128)S(1)} %copy.122, f32[128,2,8]{2,1,0:T(2,128)S(1)} %copy.120, f32[128,2,8]{2,1,0:T(2,128)S(1)} %copy.117, f32[128,2,8]{2,1,0:T(2,128)S(1)} %copy.115), kind=kOutput, calls=%fused_computation.18 | convolution fusion | flops 17563648 | bytes 2973696 | tf_op jit(solution)/shard_map/rjgl,rljd->rjgd/dot_general | solution.py:38
  37.0 0.5 copy.123
  37.5 6.0 %fusion.26 = f32[128,2880]{1,0:T(8,128)} fusion(bf16[128,1024]{0,1:T(8,128)(2,1)S(1)} %bitcast.64, bf16[1024,2880]{0,1:T(8,128)(2,1)} %param.20), kind=kOutput, calls=%fused_computation.58 | convolution fusion | flops 754974720 | bytes 7634944 | tf_op jit(solution)/shard_map/dot_general | solution.py:63
  43.6 0.2 all-gather.2.cloned.1.call-start
  44.1 0.6 reduce-window.6
  45.4 10.0 %reduce-scatter.2.cloned.1.call-done = f32[64,2880]{1,0:T(8,128)} async-done(((f32[128,2880]{1,0:T(8,128)}), f32[64,2880]{1,0:T(8,128)}) %reduce-scatter.2.cloned.1.call-update) | async-done | bytes 737296 | tf_op jit(solution)/shard_map/reduce_scatter | solution.py:62
  55.4 1.3 multiply_reduce_fusion.1
  56.8 1.3 multiply_convert_fusion.1
  58.0 1.0 convolution_convert_fusion.1
  59.0 3.0 copy.128
  62.0 74.5 %all_to_all.10 = bf16[8,64,2880]{2,1,0:T(8,128)(2,1)} all-to-all(bf16[8,64,2880]{2,1,0:T(8,128)(2,1)} %bitcast.60), channel_id=1, replica_groups=mesh['groups'=2,'att'=8,'exp'=2] {'att'}, dimensions={0} | all-to-all | bytes 5898240 | tf_op jit(solution)/shard_map/all_to_all | solution.py:94
  136.6 15.1 %all-gather.2.cloned.1.call-done = bf16[8,128,2880]{2,1,0:T(8,128)(2,1)} async-done(((bf16[8,64,2880]{2,1,0:T(8,128)(2,1)}), bf16[8,128,2880]{2,1,0:T(8,128)(2,1)}) %all-gather.2.cloned.1.call-update) | async-done | bytes 5898256 | tf_op jit(solution)/shard_map/all_gather | solution.py:95
  151.8 8.2 %fusion.1 = f32[1024,720]{0,1:T(8,128)S(1)} fusion(bf16[1024,2880]{1,0:T(8,128)(2,1)} %bitcast.68, bf16[1,2880,720]{1,2,0:T(8,128)(2,1)} %param.26), kind=kOutput, calls=%fused_computation.6 | convolution fusion | flops 4246732800 | bytes 12994560 | tf_op jit(solution)/shard_map/dot_general | solution.py:99
  160.0 5.2 %fusion.9 = bf16[90,8,8,128]{3,2,1,0:T(8,128)(2,1)S(1)} fusion(f32[1024,720]{0,1:T(8,128)S(1)} %fusion.1, bf16[1024,2880]{1,0:T(8,128)(2,1)S(1)} %bitcast.69, bf16[1,2880,720]{1,2,0:T(8,128)(2,1)S(1)} %bitcast.71), kind=kOutput, calls=%fused_computation.14 | convolution fusion | flops 4251156480 | bytes 14469120 | tf_op jit(solution)/shard_map/dot_general | solution.py:98
  165.3 7.1 %convolution_convert_fusion = bf16[8,128,2880]{2,1,0:T(8,128)(2,1)} fusion(bf16[1,720,2880]{2,1,0:T(8,128)(2,1)S(1)} %bitcast.73, bf16[90,8,8,128]{3,2,1,0:T(8,128)(2,1)S(1)} %fusion.9), kind=kOutput, calls=%fused_computation.3 | convolution fusion | flops 4249681920 | bytes 11520000 | tf_op jit(solution)/shard_map/dot_general | solution.py:101
  172.4 32.2 %all-reduce.2.cloned.1.call-done = bf16[8,128,2880]{2,1,0:T(8,128)(2,1)} async-done(((bf16[8,128,2880]{2,1,0:T(8,128)(2,1)}), bf16[8,128,2880]{2,1,0:T(8,128)(2,1)}) %all-reduce.2.cloned.1.call-update) | async-done | bytes 5898256 | tf_op jit(solution)/shard_map/psum | solution.py:104
  204.6 3.7 %convert_convert_fusion = bf16[8,64,2880]{2,1,0:T(8,128)(2,1)} fusion(bf16[8,128,2880]{2,1,0:T(8,128)(2,1)} %all-reduce.2.cloned.1.call-done, s32[]{:T(128)S(6)} %select_n.41), kind=kLoop, calls=%fused_computation.2 | loop fusion | flops 2949120 | bytes 5898244 | tf_op jit(solution)/shard_map/convert_element_type | solution.py:106
  208.3 5.8 %all-to-all-start.1 = ((bf16[8,64,2880]{2,1,0:T(8,128)(2,1)}), bf16[8,64,2880]{2,1,0:T(8,128)(2,1)S(1)}, u32[]{:S(2)}, u32[]{:S(2)}) async-start(bf16[8,64,2880]{2,1,0:T(8,128)(2,1)} %convert_convert_fusion), calls=%async_computation.2 | async-start | bytes 6029312 | tf_op jit(solution)/shard_map/all_to_all | solution.py:107
  214.7 0.4 fusion.27
  215.1 1.5 gather_fusion.1
  216.9 65.6 %all-to-all-done.1 = bf16[8,64,2880]{2,1,0:T(8,128)(2,1)S(1)} async-done(((bf16[8,64,2880]{2,1,0:T(8,128)(2,1)}), bf16[8,64,2880]{2,1,0:T(8,128)(2,1)S(1)}, u32[]{:S(2)}, u32[]{:S(2)}) %all-to-all-start.1) | async-done | bytes 2949152 | tf_op jit(solution)/shard_map/all_to_all | solution.py:107
  282.4 2.7 gather_fusion
  285.1 2.9 gather.11
  288.0 3.0 %multiply_reduce_fusion = f32[64,2880]{1,0:T(8,128)S(1)} fusion(f32[64,4]{1,0:T(8,128)S(1)} %copy.134, bf16[64,4,2880]{2,1,0:T(4,128)(2,1)S(1)} %gather.11, pred[64,4]{1,0:T(8,128)(4,1)S(1)} %copy.127), kind=kLoop, calls=%fused_computation.10 | loop fusion | flops 2764800 | bytes 2213120 | tf_op jit(solution)/shard_map/reduce_sum | solution.py:111
  291.1 0.8 add_convert_fusion
  (78 shorter events, 3.3 us)
Async XLA Ops:
  6.5 208.1 %copy-start = (f32[2880,8]{0,1:T(8,128)S(1)}, f32[2880,8]{0,1:T(8,128)}, u32[]{:S(2)}) copy-start(f32[2880,8]{0,1:T(8,128)} %param.23) | copy-start | bytes 276484
  6.5 48.9 %reduce-scatter.2.cloned.1.call-start = ((), (), s32[]{:S(2)}) async-start(), calls=%async_computation.3 | async-start | bytes 2260992 | tf_op jit(solution)/shard_map/reduce_scatter | solution.py:62
  9.9 6.5 %copy-start.4 = (bf16[128,1024]{1,0:T(8,128)(2,1)S(1)}, bf16[128,1024]{1,0:T(8,128)(2,1)}, u32[]{:S(2)}) copy-start(bf16[128,1024]{1,0:T(8,128)(2,1)} %param.14) | copy-start | bytes 786436
  20.3 6.5 %copy-start.9 = (s32[128]{0:T(128)S(1)}, s32[128]{0:T(128)}, u32[]{:S(2)}) copy-start(s32[128]{0:T(128)} %param.19) | copy-start | bytes 1540
  20.3 6.6 %copy-start.6 = (bf16[128,128]{1,0:T(8,128)(2,1)S(1)}, bf16[128,128]{1,0:T(8,128)(2,1)}, u32[]{:S(2)}) copy-start(bf16[128,128]{1,0:T(8,128)(2,1)} %param.16) | copy-start | bytes 98308
  27.2 4.7 %copy-start.7 = (bf16[128,128]{1,0:T(8,128)(2,1)S(1)}, bf16[128,128]{1,0:T(8,128)(2,1)}, u32[]{:S(2)}) copy-start(bf16[128,128]{1,0:T(8,128)(2,1)} %param.15) | copy-start | bytes 98308
  37.5 6.3 %copy-start.5 = (s32[64,4]{0,1:T(4,128)S(1)}, s32[64,4]{0,1:T(4,128)}, u32[]{:S(2)}) copy-start(s32[64,4]{0,1:T(4,128)} %param.24) | copy-start | bytes 3076
  37.5 17.9 %copy-start.2 = (bf16[64,2880]{1,0:T(8,128)(2,1)S(1)}, bf16[64,2880]{1,0:T(8,128)(2,1)}, u32[]{:S(2)}) copy-start(bf16[64,2880]{1,0:T(8,128)(2,1)} %param.21) | copy-start | bytes 1105924
  37.5 19.3 %copy-start.8 = (f32[2880]{0:T(1024)S(1)}, f32[2880]{0:T(1024)}, u32[]{:S(2)}) copy-start(f32[2880]{0:T(1024)} %param.22) | copy-start | bytes 34564
  43.6 108.2 %all-gather.2.cloned.1.call-start = ((), (), s32[]{:S(2)}) async-start(), calls=%async_computation.4 | async-start | bytes 9043968 | tf_op jit(solution)/shard_map/all_gather | solution.py:95
  136.5 23.5 %slice-start = ((s8[4239360]{0:T(1024)(128)(4,1)}), s8[45056]{0:T(1024)(128)(4,1)S(1)}, s32[]{:S(2)}) async-start(s8[4239360]{0:T(1024)(128)(4,1)} %bitcast.70), calls=%async_computation.6 | async-start | bytes 90112
  136.6 68.0 %all-reduce.2.cloned.1.call-start = ((), (), s32[]{:S(2)}) async-start(), calls=%async_computation.5 | async-start | bytes 12058624 | tf_op jit(solution)/shard_map/psum | solution.py:104
  151.8 8.3 %copy-start.10 = (bf16[8,128,2880]{2,1,0:T(8,128)(2,1)S(1)}, bf16[8,128,2880]{2,1,0:T(8,128)(2,1)}, u32[]{:S(2)}) copy-start(bf16[8,128,2880]{2,1,0:T(8,128)(2,1)} %all-gather.2.cloned.1.call-done) | copy-start | bytes 17694724
  151.8 8.3 %slice-start.1 = ((s8[4239360]{0:T(1024)(128)(4,1)}), s8[4194304]{0:T(1024)(128)(4,1)S(1)}, s32[]{:S(2)}) async-start(s8[4239360]{0:T(1024)(128)(4,1)} %bitcast.70), calls=%async_computation.7 | async-start | bytes 8388608
  151.8 13.5 %slice-start.2 = ((s8[4239360]{0:T(1024)(128)(4,1)}), s8[4194304]{0:T(1024)(128)(4,1)S(1)}, s32[]{:S(2)}) async-start(s8[4239360]{0:T(1024)(128)(4,1)} %bitcast.72), calls=%async_computation.8 | async-start | bytes 8388608
  160.0 5.2 %slice-start.3 = ((s8[4239360]{0:T(1024)(128)(4,1)}), s8[45056]{0:T(1024)(128)(4,1)S(1)}, s32[]{:S(2)}) async-start(s8[4239360]{0:T(1024)(128)(4,1)} %bitcast.72), calls=%async_computation.9 | async-start | bytes 90112
  208.3 74.1 %all-to-all-start.1 = ((bf16[8,64,2880]{2,1,0:T(8,128)(2,1)}), bf16[8,64,2880]{2,1,0:T(8,128)(2,1)S(1)}, u32[]{:S(2)}, u32[]{:S(2)}) async-start(bf16[8,64,2880]{2,1,0:T(8,128)(2,1)} %convert_convert_fusion), calls=%async_computation.2 | async-start | bytes 6029312 | tf_op jit(solution)/shard_map/all_to_all | solution.py:107
  285.1 5.9 %copy-start.1 = (f32[64,2880]{1,0:T(8,128)S(1)}, f32[64,2880]{1,0:T(8,128)}, u32[]{:S(2)}) copy-start(f32[64,2880]{1,0:T(8,128)} %reduce-scatter.2.cloned.1.call-done) | copy-start | bytes 2211844
  285.1 5.9 %copy-start.3 = (bf16[64,2880]{1,0:T(8,128)(2,1)S(1)}, bf16[64,2880]{1,0:T(8,128)(2,1)}, u32[]{:S(2)}) copy-start(bf16[64,2880]{1,0:T(8,128)(2,1)} %param.21) | copy-start | bytes 1105924
Sparse Core Ops, SparseCore 0:
  43.7 11.6 reduce-scatter.1
  136.7 15.0 all-gather.1
  172.5 31.9 all-reduce.1
where the time goes:
time: 299 us; the launch traced here: 298 us
  waiting for transfers between devices  123 us (41%)
  blocking collectives  74.5 us (25%)
  matrix products  36.1 us (12%)
  local copies, waits for them, and re-layouts  33.2 us (11%)
  between operations  13.6 us (5%)
  other arithmetic  12.1 us (4%)
  starting transfers between devices  6.05 us (2%)
    all_to_all x1, blocking collectives, per_device(): lax.all_to_all(outgoing, 'att', split_axis=0, concat_axis=0, tiled=True)  74.5 us
    all_to_all x1, waiting for transfers between devices, per_device(): lax.all_to_all(finished, 'att', split_axis=0, concat_axis=0, tiled=True)  65.6 us
    psum x1, waiting for transfers between devices, per_device(): lax.psum(partial_value.astype(jnp.bfloat16), 'exp').astype(jnp.float32)  32.2 us
    all_gather x1, waiting for transfers between devices, per_device(): routed_block = lax.all_gather(arrived, 'exp', axis=1, tiled=True)  15.1 us
    reduce_scatter x1, waiting for transfers between devices, per_device(): lax.psum_scatter(jnp.dot(attended, out_proj, preferred_element_type=jnp.f...  10 us
    dot_general x1, matrix products, per_device(): up_part = jnp.dot(flat_rows, up_matrix, preferred_element_type=jnp.float32)  8.23 us
    unnamed x36, local copies, waits for them, and re-layouts  7.23 us
    dot_general x1, matrix products, per_device(): result = jnp.dot(activated, down_matrix, preferred_element_type=jnp.float32)  7.08 us
  transfers between devices with their start and end apart: 4, of which 4 were waited for; matrix products, arithmetic and copies ran while one was open for 1% of the time, Pallas kernels for 0%

commit v1 on v0

v1 whole, which is shorter than its diff:
```python
import functools
import math

import jax
import jax.numpy as jnp
from jax import lax
from jax.experimental import pallas as pl
from jax.experimental.pallas import tpu as pltpu
from jax.sharding import PartitionSpec as P

HEAD = 64


def attend(query, new_key, new_value, cache_keys, cache_values, lengths):
    requests = query.shape[0]
    cache_len = cache_keys.shape[1]
    value_heads = new_key.shape[1] // HEAD
    group_size = query.shape[1] // new_key.shape[1]
    inverse_root = 1.0 / math.sqrt(HEAD)
    queries = query.reshape(requests, value_heads, group_size, HEAD)
    cached_k = cache_keys.reshape(requests, cache_len, value_heads, HEAD)
    cached_v = cache_values.reshape(requests, cache_len, value_heads, HEAD)
    fresh_k = new_key.reshape(requests, value_heads, HEAD)
    fresh_v = new_value.astype(jnp.float32).reshape(requests, value_heads, HEAD)
    cached_scores = (
        jnp.einsum("rjgd,rljd->rjgl", queries, cached_k, preferred_element_type=jnp.float32)
        * inverse_root
    )
    fresh_scores = (
        jnp.einsum("rjgd,rjd->rjg", queries, fresh_k, preferred_element_type=jnp.float32)
        * inverse_root
    )
    live_mask = jnp.arange(cache_len)[None, :] < lengths[:, None]
    cached_scores = jnp.where(live_mask[:, None, None, :], cached_scores, -1e30)
    highest = jnp.maximum(jnp.max(cached_scores, axis=-1), fresh_scores)
    cached_exp = jnp.exp(cached_scores - highest[..., None])
    fresh_exp = jnp.exp(fresh_scores - highest)
    totals = jnp.sum(cached_exp, axis=-1) + fresh_exp
    cached_probs = (cached_exp / totals[..., None]).astype(jnp.bfloat16)
    fresh_probs = (fresh_exp / totals).astype(jnp.bfloat16)
    output = jnp.einsum(
        "rjgl,rljd->rjgd", cached_probs, cached_v, preferred_element_type=jnp.float32
    )
    output = output + fresh_probs.astype(jnp.float32)[..., None] * fresh_v[:, :, None, :]
    return output.astype(jnp.bfloat16).reshape(requests, query.shape[1])


INNER = 2


def moe_kernel(
    depth,
    x_ref,
    hidden_ref,
    gate_hbm,
    up_hbm,
    down_hbm,
    out_ref,
    rows_buf,
    part_buf,
    mate_buf,
    side_buf,
    line_buf,
    gate_w,
    up_w,
    down_w,
    weight_sem,
    local_sem,
    rows_send,
    rows_recv,
    mate_send,
    mate_recv,
    side_send,
    side_recv,
    line_send,
    line_recv,
):
    me = lax.axis_index("att")
    core = lax.axis_index("exp")
    other = 1 - core
    line = me // INNER
    side = me % INNER
    width = hidden_ref.shape[1]
    experts = rows_buf.shape[0]
    tokens = x_ref.shape[0]
    padded = x_ref.shape[1]

    def chip(at_line, at_side):
        return at_line * INNER + at_side

    mate_id = {"exp": other}
    side_id = {"att": chip(line, 1 - side)}
    up_id = {"att": chip(jnp.minimum(line + 1, depth - 1), side)}
    down_id = {"att": chip(jnp.maximum(line - 1, 0), side)}
    has_up = line + 1 < depth
    has_down = line >= 1
    mesh_ids = pl.DeviceIdType.MESH

    barrier = pltpu.get_barrier_semaphore()
    pl.semaphore_signal(barrier, inc=1, device_id=mate_id, device_id_type=mesh_ids)
    pl.semaphore_signal(barrier, inc=1, device_id=side_id, device_id_type=mesh_ids)

    @pl.when(has_up)
    def _():
        pl.semaphore_signal(barrier, inc=1, device_id=up_id, device_id_type=mesh_ids)

    @pl.when(has_down)
    def _():
        pl.semaphore_signal(barrier, inc=1, device_id=down_id, device_id_type=mesh_ids)

    loads = [
        pltpu.make_async_copy(gate_hbm.at[0], gate_w, weight_sem.at[0]),
        pltpu.make_async_copy(up_hbm.at[0], up_w, weight_sem.at[1]),
        pltpu.make_async_copy(down_hbm.at[0], down_w, weight_sem.at[2]),
    ]
    own_copy = pltpu.make_async_copy(x_ref, rows_buf.at[me, core], local_sem)
    own_copy.start()
    for load in loads:
        load.start()
    own_copy.wait()
    pl.semaphore_wait(barrier, 2 + has_up.astype(jnp.int32) + has_down.astype(jnp.int32))

    def rows_copy(block, kind, target):
        return pltpu.make_async_remote_copy(
            src_ref=rows_buf.at[block, core],
            dst_ref=rows_buf.at[block, core],
            send_sem=rows_send.at[block, kind],
            recv_sem=rows_recv.at[block, core],
            device_id=target,
            device_id_type=mesh_ids,
        )

    def rows_arrived(block, lane):
        pltpu.make_async_remote_copy(
            src_ref=rows_buf.at[block, lane],
            dst_ref=rows_buf.at[block, lane],
            send_sem=rows_send.at[block, 0],
            recv_sem=rows_recv.at[block, lane],
            device_id=mate_id,
            device_id_type=mesh_ids,
        ).wait_recv()

    def mate_copy(block):
        return pltpu.make_async_remote_copy(
            src_ref=part_buf.at[block, other],
            dst_ref=mate_buf.at[block],
            send_sem=mate_send.at[block],
            recv_sem=mate_recv.at[block],
            device_id=mate_id,
            device_id_type=mesh_ids,
        )

    def side_copy(at_line):
        return pltpu.make_async_remote_copy(
            src_ref=part_buf.at[chip(at_line, 1 - side), core],
            dst_ref=side_buf.at[at_line],
            send_sem=side_send.at[at_line],
            recv_sem=side_recv.at[at_line],
            device_id=side_id,
            device_id_type=mesh_ids,
        )

    def line_copy(at_line, way, target):
        return pltpu.make_async_remote_copy(
            src_ref=part_buf.at[chip(at_line, side), core],
            dst_ref=line_buf.at[way, at_line],
            send_sem=line_send.at[at_line],
            recv_sem=line_recv.at[way, at_line],
            device_id=target,
            device_id_type=mesh_ids,
        )

    def place(step, way):
        at_line = jnp.where(way == 0, line - step, line + step)
        exists = (at_line >= 0) & (at_line < depth) & ((step > 0) | (way == 0))
        exists = exists & (step >= 0) & (step < depth)
        return jnp.clip(at_line, 0, depth - 1), exists

    def expert(block):
        rows = rows_buf[block].reshape(2 * tokens, padded)
        values = rows[:, :width]
        first = (width // 128) * 128
        tail = rows[:, first:].astype(jnp.float32)
        lanes = lax.broadcasted_iota(jnp.int32, tail.shape, 1) + first - width
        chosen = (lanes == me) | (lanes == me + experts)
        weight = jnp.sum(jnp.where(chosen, tail, 0.0), axis=1, keepdims=True)
        gate = jnp.dot(values, gate_w[...], preferred_element_type=jnp.float32)
        up = jnp.dot(values, up_w[...], preferred_element_type=jnp.float32)
        activated = (gate / (1.0 + jnp.exp(-gate)) * up).astype(jnp.bfloat16)
        result = jnp.dot(activated, down_w[...], preferred_element_type=jnp.float32)
        result = (result * weight).astype(jnp.bfloat16)
        part_buf[block] = result.reshape(2, tokens, width)
        mate_copy(block).start()

    def gather_step(step, carry):
        def relay_line(way, inner):
            at_line, exists = place(step, way)
            block = chip(at_line, side)

            @pl.when(exists)
            def _():
                @pl.when(step > 0)
                def _():
                    rows_arrived(block, core)

                @pl.when(has_up & (at_line <= line))
                def _():
                    rows_copy(block, 2, up_id).start()

                @pl.when(has_down & (at_line >= line))
                def _():
                    rows_copy(block, 3, down_id).start()

                rows_copy(block, 1, side_id).start()
                rows_copy(block, 0, mate_id).start()

            return inner

        def relay_side(way, inner):
            at_line, exists = place(step - 1, way)
            block = chip(at_line, 1 - side)

            @pl.when(exists)
            def _():
                rows_arrived(block, core)
                rows_copy(block, 0, mate_id).start()

            return inner

        lax.fori_loop(0, 2, relay_line, 0)
        lax.fori_loop(0, 2, relay_side, 0)

        @pl.when(step == 0)
        def _():
            for load in loads:
                load.wait()

        def compute(index, inner):
            way = index % 2
            mine = index // 2
            at_line, exists = place(step - mine, way)
            block = chip(at_line, jnp.where(mine == 0, side, 1 - side))

            @pl.when(exists)
            def _():
                rows_arrived(block, other)
                expert(block)

            return inner

        lax.fori_loop(0, 4, compute, 0)
        return carry

    lax.fori_loop(0, depth + 1, gather_step, 0)

    def side_step(index, carry):
        step = depth - 1 - index // 2
        at_line, exists = place(step, index % 2)
        block = chip(at_line, 1 - side)

        @pl.when(exists)
        def _():
            mate_copy(block).wait_recv()
            total = part_buf[block, core].astype(jnp.float32) + mate_buf[block].astype(jnp.float32)
            part_buf[block, core] = total.astype(jnp.bfloat16)
            side_copy(at_line).start()

        return carry

    lax.fori_loop(0, 2 * depth, side_step, 0)

    def line_total(at_line):
        block = chip(at_line, side)
        mate_copy(block).wait_recv()
        side_copy(at_line).wait_recv()
        total = part_buf[block, core].astype(jnp.float32) + mate_buf[block].astype(jnp.float32)
        return total + side_buf[at_line].astype(jnp.float32)

    def line_step(index, carry):
        step = depth - 1 - index // 2
        at_line, exists = place(step, index % 2)
        block = chip(at_line, side)

        @pl.when(exists)
        def _():
            upward = at_line > line
            way = jnp.where(upward, 0, 1)
            feeds = jnp.where(upward, has_down, has_up)

            part_buf[block, core] = line_total(at_line).astype(jnp.bfloat16)

            @pl.when(feeds)
            def _():
                line_copy(at_line, way, up_id).wait_recv()
                total = part_buf[block, core].astype(jnp.float32)
                total = total + line_buf[way, at_line].astype(jnp.float32)
                part_buf[block, core] = total.astype(jnp.bfloat16)

            @pl.when(upward)
            def _():
                line_copy(at_line, 0, up_id).start()

            @pl.when(jnp.logical_not(upward))
            def _():
                line_copy(at_line, 1, down_id).start()

        return carry

    lax.fori_loop(0, 2 * (depth - 1), line_step, 0)

    hidden_ref[...] = hidden_ref[...] + line_total(line)

    @pl.when(has_down)
    def _():
        line_copy(line, 0, up_id).wait_recv()
        hidden_ref[...] = hidden_ref[...] + line_buf[0, line].astype(jnp.float32)

    @pl.when(has_up)
    def _():
        line_copy(line, 1, up_id).wait_recv()
        hidden_ref[...] = hidden_ref[...] + line_buf[1, line].astype(jnp.float32)

    out_ref[...] = hidden_ref[...].astype(out_ref.dtype)

    def drain(at_line, carry):
        block = chip(at_line, side)
        across = chip(at_line, 1 - side)
        rows_copy(block, 0, mate_id).wait_send()
        rows_copy(block, 1, side_id).wait_send()
        rows_copy(across, 0, mate_id).wait_send()

        @pl.when(has_up & (at_line <= line))
        def _():
            rows_copy(block, 2, up_id).wait_send()

        @pl.when(has_down & (at_line >= line))
        def _():
            rows_copy(block, 3, down_id).wait_send()

        mate_copy(block).wait_send()
        mate_copy(across).wait_send()
        side_copy(at_line).wait_send()

        @pl.when(at_line != line)
        def _():
            line_copy(at_line, 0, up_id).wait_send()

        return carry

    lax.fori_loop(0, depth, drain, 0)


def routed_experts(rows, hidden_state, w_gate, w_up, w_down):
    experts = lax.axis_size("att")
    depth = experts // INNER
    tokens, padded = rows.shape
    width = hidden_state.shape[1]
    inner = w_gate.shape[2]
    bf16 = jnp.bfloat16
    dma = pltpu.SemaphoreType.DMA
    vmem = pl.BlockSpec(memory_space=pltpu.VMEM)
    hbm = pl.BlockSpec(memory_space=pl.ANY)

    def body(*refs):
        x_ref, hidden_in, *rest = refs
        hidden = rest[-1]
        hidden[...] = hidden_in[...]
        moe_kernel(depth, x_ref, hidden, *rest[:-1])

    return pl.pallas_call(
        body,
        out_shape=jax.ShapeDtypeStruct((tokens, width), bf16),
        in_specs=[vmem, vmem, hbm, hbm, hbm],
        out_specs=vmem,
        scratch_shapes=[
            pltpu.VMEM((experts, 2, tokens, padded), bf16),
            pltpu.VMEM((experts, 2, tokens, width), bf16),
            pltpu.VMEM((experts, tokens, width), bf16),
            pltpu.VMEM((depth, tokens, width), bf16),
            pltpu.VMEM((2, depth, tokens, width), bf16),
            pltpu.VMEM((width, inner), bf16),
            pltpu.VMEM((width, inner), bf16),
            pltpu.VMEM((inner, width), bf16),
            dma((3,)),
            dma,
            dma((experts, 4)),
            dma((experts, 2)),
            dma((experts,)),
            dma((experts,)),
            dma((depth,)),
            dma((depth,)),
            dma((depth,)),
            dma((2, depth)),
            pltpu.VMEM((tokens, width), jnp.float32),
        ],
        compiler_params=pltpu.CompilerParams(
            collective_id=0, has_side_effects=True, vmem_limit_bytes=62 * 1024 * 1024
        ),
    )(rows, hidden_state, w_gate, w_up, w_down)


def per_device(
    query,
    new_key,
    new_value,
    cache_keys,
    cache_values,
    lengths,
    out_proj,
    residual,
    norm_gain,
    router,
    routes,
    w_gate,
    w_up,
    w_down,
):
    attended = attend(query, new_key, new_value, cache_keys, cache_values, lengths)
    summed = lax.psum_scatter(
        jnp.dot(attended, out_proj, preferred_element_type=jnp.float32),
        "exp",
        scatter_dimension=0,
        tiled=True,
    )
    hidden_state = residual.astype(jnp.float32) + summed
    mean_square = jnp.mean(hidden_state * hidden_state, axis=-1, keepdims=True)
    normed = (hidden_state * lax.rsqrt(mean_square + 1e-05) * norm_gain).astype(jnp.bfloat16)
    logits = jnp.dot(normed.astype(jnp.float32), router, precision=lax.Precision.HIGHEST)
    experts = lax.axis_size("att")
    named = jnp.any(routes[:, :, None] == jnp.arange(experts)[None, None, :], axis=1)
    squashed = jnp.where(named, jax.nn.sigmoid(logits), 0.0)
    gate_weights = squashed / jnp.sum(squashed, axis=1, keepdims=True)
    coarse = lax.reduce_precision(gate_weights, 8, 7)
    fine = (gate_weights - coarse).astype(jnp.bfloat16)
    width = normed.shape[1]
    spare = pl.cdiv(width + 2 * experts, 128) * 128 - width - 2 * experts
    rows = jnp.concatenate(
        [normed, coarse.astype(jnp.bfloat16), fine, jnp.zeros((normed.shape[0], spare), jnp.bfloat16)],
        axis=1,
    )
    return routed_experts(rows, hidden_state, w_gate, w_up, w_down)


def solution(mesh):
    in_specs = (
        P(("groups", "att"), "exp"),
        P(("groups", "att"), "exp"),
        P(("groups", "att"), "exp"),
        P(("groups", "att"), None, "exp"),
        P(("groups", "att"), None, "exp"),
        P(("groups", "att")),
        P("exp", None),
        P(("groups", "att", "exp"), None),
        P(),
        P(),
        P(("groups", "att", "exp"), None),
        P("att", None, "exp"),
        P("att", None, "exp"),
        P("att", "exp", None),
    )
    out_specs = P(("groups", "att", "exp"), None)
    return jax.shard_map(
        per_device, mesh=mesh, in_specs=in_specs, out_specs=out_specs, check_vma=False
    )
```

time: 299 us -> 156 us (0.52)
  waiting for transfers between devices: 123 us -> 0.02 us
  Pallas kernels: 0 us -> 81.4 us
  blocking collectives: 74.5 us -> 0 us
  matrix products: 36.1 us -> 14.9 us
  other arithmetic: 12.1 us -> 3.23 us
  local copies, waits for them, and re-layouts: 33.2 us -> 41.9 us
  starting transfers between devices: 6.05 us -> 0.01 us
    pallas_call x0 -> x1, Pallas kernels: none -> 81.4 us  [routed_experts(): pl.pallas_call(body, out_shape=jax.ShapeDtypeStruct((tokens, width), bf16...]
    all_to_all x1 -> x0, blocking collectives: 74.5 us -> none  [per_device(): lax.all_to_all(outgoing, 'att', split_axis=0, concat_axis=0, tiled=True)]
    all_to_all x1 -> x0, waiting for transfers between devices: 65.6 us -> none  [per_device(): lax.all_to_all(finished, 'att', split_axis=0, concat_axis=0, tiled=True)]
    psum x1 -> x0, waiting for transfers between devices: 32.2 us -> none  [per_device(): lax.psum(partial_value.astype(jnp.bfloat16), 'exp').astype(jnp.float32)]
    dot_general x4 -> x0, matrix products: 21.5 us -> none  [the longest x1 8.23 us: per_device(): up_part = jnp.dot(flat_rows, up_matrix, preferred_element_type=jnp.float32)]
    unnamed x36 -> x18, local copies, waits for them, and re-layouts: 7.23 us -> 24.4 us
    all_gather x1 -> x0, waiting for transfers between devices: 15.1 us -> none  [per_device(): routed_block = lax.all_gather(arrived, 'exp', axis=1, tiled=True)]
    reduce_scatter x1, waiting for transfers between devices: 10 us -> 0.01 us  [per_device(): lax.psum_scatter(jnp.dot(attended, out_proj, preferred_element_type=jnp.f...]
  transfers between devices with their start and end apart: 4 -> 1, of which waited for: 4 -> 0; matrix products, arithmetic and copies ran while one was open for 1% -> 9% of each run, Pallas kernels for 0% -> 0%
where the time goes in v1:
time: 156 us; the launch traced here: 155 us
  Pallas kernels  81.4 us (52%)
  local copies, waits for them, and re-layouts  41.9 us (27%)
  matrix products  14.9 us (10%)
  between operations  13.6 us (9%)
  other arithmetic  3.23 us (2%)
    pallas_call x1, Pallas kernels, routed_experts(): pl.pallas_call(body, out_shape=jax.ShapeDtypeStruct((tokens, width), bf16...  81.4 us
    unnamed x18, local copies, waits for them, and re-layouts  24.4 us
    reshape x1, local copies, waits for them, and re-layouts, attend(): cached_k = cache_keys.reshape(requests, cache_len, value_heads, HEAD)  6.47 us
    reshape x1, local copies, waits for them, and re-layouts, attend(): cached_v = cache_values.reshape(requests, cache_len, value_heads, HEAD)  6.47 us
    dot_general x1, matrix products, per_device(): jnp.dot(attended, out_proj, preferred_element_type=jnp.float32)  6.02 us
    dot_general x1, matrix products, attend(): jnp.einsum('rjgd,rljd->rjgl', queries, cached_k, preferred_element_type=j...  4.79 us
    dot_general x1, matrix products, attend(): jnp.einsum('rjgl,rljd->rjgd', cached_probs, cached_v, preferred_element_t...  3.55 us
  transfers between devices with their start and end apart: 1, of which 0 were waited for; matrix products, arithmetic and copies ran while one was open for 9% of the time, Pallas kernels for 0%

profile of v1, /device:TPU:0, one launch (start us, length us, event | category | flops | bytes accessed | tf_op | source)
XLA Modules:
  0.0 155.1 jit_solution(13692535961455344950)
XLA Ops:
  6.5 0.8 iota_compare_fusion
  7.3 0.9 copy.71
  8.2 0.9 copy.79
  9.1 0.1 copy.80
  9.2 1.1 copy.67
  10.3 0.1 multiply_reduce_fusion.1
  10.4 1.2 copy.69
  11.6 3.3 %copy.68 = bf16[128,64,128]{0,2,1:T(8,128)(2,1)S(1)} copy(bf16[128,64,128]{2,1,0:T(8,128)(2,1)} %param.17) | data formatting | bytes 4194304 | tf_op args[3]
  14.9 6.5 %copy.70 = bf16[128,64,2,64]{3,1,2,0:T(8,128)(2,1)} copy(bf16[128,64,2,64]{0,3,2,1:T(8,128)(2,1)S(1)} %bitcast.19) | data formatting | bytes 4194304 | tf_op jit(solution)/shard_map/reshape | solution.py:21
  21.4 4.8 %fusion.13 = (f32[128,2,8]{2,1,0:T(2,128)S(1)}, f32[128,2,8,64]{3,2,1,0:T(8,128)S(1)}) fusion(bf16[128,2,8,64]{3,2,1,0:T(8,128)(2,1)} %copy.69, bf16[128,64,2,64]{3,1,2,0:T(8,128)(2,1)} %copy.70, pred[128,64]{1,0:T(8,128)(4,1)S(1)} %iota_compare_fusion), kind=kOutput, calls=%fused_computation.32 | convolution fusion | flops 17168384 | bytes 2899968 | tf_op jit(solution)/shard_map/rjgd,rljd->rjgl/dot_general | solution.py:26
  26.2 0.1 copy.72
  26.3 0.2 copy.73
  26.4 0.8 fusion.6
  27.2 0.1 copy.74
  27.3 0.8 copy.75
  28.1 0.8 copy.78
  28.9 3.3 %copy.76 = bf16[128,64,128]{0,2,1:T(8,128)(2,1)S(1)} copy(bf16[128,64,128]{2,1,0:T(8,128)(2,1)} %param.18) | data formatting | bytes 4194304 | tf_op args[4]
  32.2 6.5 %copy.77 = bf16[128,64,2,64]{3,1,2,0:T(8,128)(2,1)} copy(bf16[128,64,2,64]{0,3,2,1:T(8,128)(2,1)S(1)} %bitcast.20) | data formatting | bytes 4194304 | tf_op jit(solution)/shard_map/reshape | solution.py:22
  38.7 3.6 %fusion.1 = bf16[128,2,8,64]{3,2,1,0:T(8,128)(2,1)S(1)} fusion(bf16[128,64,2,64]{3,1,2,0:T(8,128)(2,1)} %copy.77, f32[128,2,8,64]{3,2,1,0:T(8,128)S(1)} %get-tuple-element.12, f32[128,2,64]{2,1,0:T(2,128)S(1)} %copy.80, f32[128,2,8]{2,1,0:T(2,128)} %copy.78, f32[128,2,8]{2,1,0:T(2,128)} %copy.75, f32[128,2,8]{2,1,0:T(2,128)S(1)} %copy.73), kind=kOutput, calls=%fused_computation.3 | convolution fusion | flops 17563648 | bytes 2973696 | tf_op jit(solution)/shard_map/rjgl,rljd->rjgd/dot_general | solution.py:41
  42.2 0.5 copy.81
  42.7 6.0 %fusion.15 = f32[128,2880]{1,0:T(8,128)} fusion(bf16[128,1024]{0,1:T(8,128)(2,1)S(1)} %bitcast.22, bf16[1024,2880]{0,1:T(8,128)(2,1)} %param.20), kind=kOutput, calls=%fused_computation.34 | convolution fusion | flops 754974720 | bytes 7634944 | tf_op jit(solution)/shard_map/dot_general | solution.py:420
  48.7 0.0 reduce-scatter.2.cloned.1.call-update
  48.8 0.1 copy.83
  48.9 6.5 %copy.85.refs_2_ = bf16[1,2880,720]{2,1,0:T(8,128)(2,1)} copy(bf16[1,2880,720]{1,2,0:T(8,128)(2,1)} %param.25) | data formatting | bytes 8294400 | tf_op args[11]
  55.4 6.6 %copy.86.refs_3_ = bf16[1,2880,720]{2,1,0:T(8,128)(2,1)} copy(bf16[1,2880,720]{1,2,0:T(8,128)(2,1)} %param.26) | data formatting | bytes 8294400 | tf_op args[12]
  62.0 1.3 multiply_reduce_fusion
  63.4 0.1 multiply_convert_fusion
  63.5 0.6 fusion.14
  64.1 0.1 fusion.9
  64.2 0.8 concatenate.3.refs_0_
  65.1 81.4 %shard_map.136 = bf16[64,2880]{1,0:T(8,128)(2,1)} custom-call(bf16[64,2944]{1,0:T(8,128)(2,1)} %concatenate.3.refs_0_, f32[64,2880]{1,0:T(8,128)} %copy-done.1, bf16[1,2880,720]{2,1,0:T(8,128)(2,1)} %copy.85.refs_2_, bf16[1,2880,720]{2,1,0:T(8,128)(2,1)} %copy.86.refs_3_, bf16[1,720,2880]{2,1,0:T(8,128)(2,1)} %refs_4_.1), custom_call_target="tpu_custom_call" | custom-call | tf_op jit(solution)/shard_map/pallas_call | solution.py:370
  146.5 1.8 %copy.96 = bf16[64,2880]{1,0:T(8,128)(2,1)} copy(bf16[64,2880]{1,0:T(8,128)(2,1)} %shard_map.136) | data formatting | bytes 737280
  (18 shorter events, 0.1 us)
Async XLA Ops:
  6.5 57.0 %copy-start = (f32[2880,8]{0,1:T(8,128)S(1)}, f32[2880,8]{0,1:T(8,128)}, u32[]{:S(2)}) copy-start(f32[2880,8]{0,1:T(8,128)} %param.23) | copy-start | bytes 276484
  6.5 55.5 %reduce-scatter.2.cloned.1.call-start = ((), (), s32[]{:S(2)}) async-start(), calls=%async_computation.1 | async-start | bytes 2260992 | tf_op jit(solution)/shard_map/reduce_scatter | solution.py:419
  42.7 6.1 %copy-start.4 = (s32[64,4]{0,1:T(4,128)S(1)}, s32[64,4]{0,1:T(4,128)}, u32[]{:S(2)}) copy-start(s32[64,4]{0,1:T(4,128)} %param.24) | copy-start | bytes 3076
  55.4 6.6 %copy-start.2 = (bf16[64,2880]{1,0:T(8,128)(2,1)S(1)}, bf16[64,2880]{1,0:T(8,128)(2,1)}, u32[]{:S(2)}) copy-start(bf16[64,2880]{1,0:T(8,128)(2,1)} %param.21) | copy-start | bytes 1105924
  55.4 8.0 %copy-start.3 = (f32[2880]{0:T(1024)S(1)}, f32[2880]{0:T(1024)}, u32[]{:S(2)}) copy-start(f32[2880]{0:T(1024)} %param.22) | copy-start | bytes 34564
  63.4 1.7 %copy-start.1 = (f32[64,2880]{1,0:T(8,128)}, f32[64,2880]{1,0:T(8,128)S(1)}, u32[]{:S(2)}) copy-start(f32[64,2880]{1,0:T(8,128)S(1)} %get-tuple-element.6.refs_1_) | copy-start | bytes 2211844
Sparse Core Ops, SparseCore 0:
  48.9 11.6 reduce-scatter.1

commit v2 on v1

--- a/solution.py
+++ b/solution.py
@@ -1,4 +1,3 @@
-import functools
 import math
 
 import jax
@@ -9,43 +8,11 @@
 from jax.sharding import PartitionSpec as P
 
 HEAD = 64
-
-
-def attend(query, new_key, new_value, cache_keys, cache_values, lengths):
-    requests = query.shape[0]
-    cache_len = cache_keys.shape[1]
-    value_heads = new_key.shape[1] // HEAD
-    group_size = query.shape[1] // new_key.shape[1]
-    inverse_root = 1.0 / math.sqrt(HEAD)
-    queries = query.reshape(requests, value_heads, group_size, HEAD)
-    cached_k = cache_keys.reshape(requests, cache_len, value_heads, HEAD)
-    cached_v = cache_values.reshape(requests, cache_len, value_heads, HEAD)
-    fresh_k = new_key.reshape(requests, value_heads, HEAD)
-    fresh_v = new_value.astype(jnp.float32).reshape(requests, value_heads, HEAD)
-    cached_scores = (
-        jnp.einsum("rjgd,rljd->rjgl", queries, cached_k, preferred_element_type=jnp.float32)
-        * inverse_root
-    )
-    fresh_scores = (
-        jnp.einsum("rjgd,rjd->rjg", queries, fresh_k, preferred_element_type=jnp.float32)
-        * inverse_root
-    )
-    live_mask = jnp.arange(cache_len)[None, :] < lengths[:, None]
-    cached_scores = jnp.where(live_mask[:, None, None, :], cached_scores, -1e30)
-    highest = jnp.maximum(jnp.max(cached_scores, axis=-1), fresh_scores)
-    cached_exp = jnp.exp(cached_scores - highest[..., None])
-    fresh_exp = jnp.exp(fresh_scores - highest)
-    totals = jnp.sum(cached_exp, axis=-1) + fresh_exp
-    cached_probs = (cached_exp / totals[..., None]).astype(jnp.bfloat16)
-    fresh_probs = (fresh_exp / totals).astype(jnp.bfloat16)
-    output = jnp.einsum(
-        "rjgl,rljd->rjgd", cached_probs, cached_v, preferred_element_type=jnp.float32
-    )
-    output = output + fresh_probs.astype(jnp.float32)[..., None] * fresh_v[:, :, None, :]
-    return output.astype(jnp.bfloat16).reshape(requests, query.shape[1])
-
-
 INNER = 2
+
+
+def dot_t(left, right):
+    return lax.dot_general(left, right, (((1,), (1,)), ((), ())), preferred_element_type=jnp.float32)
 
 
 def moe_kernel(
@@ -184,8 +151,8 @@
         lanes = lax.broadcasted_iota(jnp.int32, tail.shape, 1) + first - width
         chosen = (lanes == me) | (lanes == me + experts)
         weight = jnp.sum(jnp.where(chosen, tail, 0.0), axis=1, keepdims=True)
-        gate = jnp.dot(values, gate_w[...], preferred_element_type=jnp.float32)
-        up = jnp.dot(values, up_w[...], preferred_element_type=jnp.float32)
+        gate = dot_t(values, gate_w[...])
+        up = dot_t(values, up_w[...])
         activated = (gate / (1.0 + jnp.exp(-gate)) * up).astype(jnp.bfloat16)
         result = jnp.dot(activated, down_w[...], preferred_element_type=jnp.float32)
         result = (result * weight).astype(jnp.bfloat16)
@@ -378,8 +345,8 @@
             pltpu.VMEM((experts, tokens, width), bf16),
             pltpu.VMEM((depth, tokens, width), bf16),
             pltpu.VMEM((2, depth, tokens, width), bf16),
-            pltpu.VMEM((width, inner), bf16),
-            pltpu.VMEM((width, inner), bf16),
+            pltpu.VMEM((inner, width), bf16),
+            pltpu.VMEM((inner, width), bf16),
             pltpu.VMEM((inner, width), bf16),
             dma((3,)),
             dma,
@@ -396,7 +363,254 @@
         compiler_params=pltpu.CompilerParams(
             collective_id=0, has_side_effects=True, vmem_limit_bytes=62 * 1024 * 1024
         ),
-    )(rows, hidden_state, w_gate, w_up, w_down)
+    )(rows, hidden_state, jnp.swapaxes(w_gate, 1, 2), jnp.swapaxes(w_up, 1, 2), w_down)
+
+
+def attend_block(query, new_key, new_value, keys, values, lengths):
+    rows = query.shape[0]
+    heads = query.shape[1] // HEAD
+    lane_heads = new_key.shape[1] // HEAD
+    group = heads // lane_heads
+    cache_len = keys.shape[1]
+    pair = 2 * HEAD
+    inverse_root = 1.0 / math.sqrt(HEAD)
+    lanes = lax.broadcasted_iota(jnp.int32, (rows, pair), 1)
+    low = lanes < HEAD
+    pieces = []
+    for head in range(heads):
+        tile = query[:, (head // 2) * pair : (head // 2 + 1) * pair]
+        lane_head = head // group
+        if head % 2 != lane_head:
+            tile = pltpu.roll(tile, HEAD, 1)
+        pieces.append(jnp.where(low if lane_head == 0 else jnp.logical_not(low), tile, 0.0))
+    stacked = jnp.concatenate(pieces, axis=0)
+    tall_key = jnp.concatenate([new_key] * heads, axis=0)
+    tall_value = jnp.concatenate([new_value] * heads, axis=0)
+    tall_length = jnp.concatenate([lengths] * heads, axis=0)
+    fresh = jnp.sum(stacked * tall_key, axis=1, keepdims=True) * inverse_root
+    scores = dot_t(stacked.astype(jnp.bfloat16), keys.reshape(rows * cache_len, pair)) * inverse_root
+    position = lax.broadcasted_iota(jnp.int32, scores.shape, 1)
+    row = lax.broadcasted_iota(jnp.int32, (scores.shape[0], 1), 0)
+    start = (row % rows) * cache_len
+    live = (position >= start) & (position < start + tall_length)
+    scores = jnp.where(live, scores, -1e30)
+    highest = jnp.maximum(jnp.max(scores, axis=1, keepdims=True), fresh)
+    cached_exp = jnp.exp(scores - highest)
+    fresh_exp = jnp.exp(fresh - highest)
+    scale = 1.0 / (jnp.sum(cached_exp, axis=1, keepdims=True) + fresh_exp)
+    probs = (cached_exp * scale).astype(jnp.bfloat16)
+    fresh_probs = (fresh_exp * scale).astype(jnp.bfloat16).astype(jnp.float32)
+    output = jnp.dot(
+        probs, values.reshape(rows * cache_len, pair), preferred_element_type=jnp.float32
+    )
+    output = output + fresh_probs * tall_value
+    tiles = []
+    for at in range(heads // 2):
+        first = output[2 * at * rows : (2 * at + 1) * rows]
+        second = output[(2 * at + 1) * rows : (2 * at + 2) * rows]
+        if (2 * at) // group == 0:
+            second = pltpu.roll(second, HEAD, 1)
+        else:
+            first = pltpu.roll(first, HEAD, 1)
+        tiles.append(jnp.where(low, first, second))
+    return jnp.concatenate(tiles, axis=1)
+
+
+STEP = 16
+HALF = 8
+SPAN = 768
+
+
+def attention_kernel(
+    experts,
+    query_ref,
+    new_key_ref,
+    new_value_ref,
+    lengths_ref,
+    residual_ref,
+    gain_ref,
+    router_ref,
+    routes_ref,
+    keys_hbm,
+    values_hbm,
+    proj_hbm,
+    rows_ref,
+    hidden_ref,
+    keys_buf,
+    values_buf,
+    proj_w,
+    attended,
+    sent,
+    landed,
+    wide_router,
+    keys_sem,
+    values_sem,
+    proj_sem,
+    send_sem,
+    recv_sem,
+):
+    core = lax.axis_index("exp")
+    other = 1 - core
+    mate = {"exp": other}
+    barrier = pltpu.get_barrier_semaphore()
+    pl.semaphore_signal(barrier, inc=1, device_id=mate, device_id_type=pl.DeviceIdType.MESH)
+    requests = query_ref.shape[0]
+    tokens, width = residual_ref.shape
+    steps = requests // STEP
+
+    def cache_load(step):
+        span = pl.ds(step * STEP, STEP)
+        return (
+            pltpu.make_async_copy(keys_hbm.at[span], keys_buf.at[span], keys_sem.at[step]),
+            pltpu.make_async_copy(values_hbm.at[span], values_buf.at[span], values_sem.at[step]),
+        )
+
+    proj_load = pltpu.make_async_copy(proj_hbm, proj_w, proj_sem)
+    for step in range(steps):
+        for load in cache_load(step):
+            load.start()
+    proj_load.start()
+
+    first = (width // 128) * 128
+    base = width - first
+    wide_router[...] = jnp.zeros_like(wide_router)
+    wide_router[base : base + experts, :] = router_ref[...]
+    wide_router[base + experts : base + 2 * experts, :] = router_ref[...]
+
+    def attend_step(step, carry):
+        span = pl.ds(pl.multiple_of(step * STEP, STEP), STEP)
+        for load in cache_load(step):
+            load.wait()
+        query = query_ref[span, :].astype(jnp.float32)
+        new_key = new_key_ref[span, :].astype(jnp.float32)
+        new_value = new_value_ref[span, :].astype(jnp.float32)
+        lengths = lengths_ref[span, :]
+        keys = keys_buf[span]
+        values = values_buf[span]
+        parts = []
+        for half in range(STEP // HALF):
+            cut = slice(half * HALF, (half + 1) * HALF)
+            parts.append(
+                attend_block(
+                    query[cut], new_key[cut], new_value[cut], keys[cut], values[cut], lengths[cut]
+                )
+            )
+        attended[span, :] = jnp.concatenate(parts, axis=0).astype(jnp.bfloat16)
+        return carry
+
+    lax.fori_loop(0, steps, attend_step, 0)
+
+    proj_load.wait()
+    pl.semaphore_wait(barrier, 1)
+    theirs = attended[pl.ds(pl.multiple_of(other * tokens, tokens), tokens), :]
+    mine = attended[pl.ds(pl.multiple_of(core * tokens, tokens), tokens), :]
+    both = jnp.concatenate([theirs, mine], axis=0)
+    copies = []
+    for at, begin in enumerate(range(0, width, SPAN)):
+        end = min(begin + SPAN, width)
+        product = dot_t(both, proj_w[begin:end, :])
+        sent[at, :, : end - begin] = product[:tokens]
+        copy = pltpu.make_async_remote_copy(
+            src_ref=sent.at[at],
+            dst_ref=landed.at[at],
+            send_sem=send_sem.at[at],
+            recv_sem=recv_sem.at[at],
+            device_id=mate,
+            device_id_type=pl.DeviceIdType.MESH,
+        )
+        copy.start()
+        copies.append(copy)
+        hidden_ref[:, begin:end] = (
+            residual_ref[:, begin:end].astype(jnp.float32) + product[tokens:]
+        )
+    squares = jnp.zeros((tokens, 1), jnp.float32)
+    for at, begin in enumerate(range(0, width, SPAN)):
+        end = min(begin + SPAN, width)
+        copies[at].wait_recv()
+        total = hidden_ref[:, begin:end] + landed[at, :, : end - begin]
+        hidden_ref[:, begin:end] = total
+        squares = squares + jnp.sum(total * total, axis=1, keepdims=True)
+    scale = lax.rsqrt(squares / width + 1e-05)
+    normed = (hidden_ref[...] * scale * gain_ref[...]).astype(jnp.bfloat16)
+    logits = lax.dot_general(
+        normed.astype(jnp.float32),
+        wide_router[...],
+        (((1,), (1,)), ((), ())),
+        precision=lax.Precision.HIGHEST,
+        preferred_element_type=jnp.float32,
+    )
+    lane = lax.broadcasted_iota(jnp.int32, logits.shape, 1) - base
+    coarse_lane = (lane >= 0) & (lane < experts)
+    fine_lane = (lane >= experts) & (lane < 2 * experts)
+    expert = jnp.where(fine_lane, lane - experts, lane)
+    named = jnp.zeros(logits.shape, jnp.bool_)
+    for at in range(routes_ref.shape[1]):
+        named = named | (routes_ref[:, at : at + 1] == expert)
+    squashed = jnp.where(named, 1.0 / (1.0 + jnp.exp(-logits)), 0.0)
+    totals = jnp.sum(jnp.where(coarse_lane, squashed, 0.0), axis=1, keepdims=True)
+    weight = squashed / totals
+    coarse = weight.astype(jnp.bfloat16).astype(jnp.float32)
+    tail = jnp.where(coarse_lane, coarse, jnp.where(fine_lane, weight - coarse, 0.0))
+    rows_ref[:, :width] = normed
+    rows_ref[:, width:] = tail[:, base:].astype(jnp.bfloat16)
+    for copy in copies:
+        copy.wait_send()
+
+
+def attention_layer(
+    query, new_key, new_value, cache_keys, cache_values, lengths, out_proj, residual, gain, router, routes
+):
+    experts = lax.axis_size("att")
+    requests = query.shape[0]
+    tokens, width = residual.shape
+    padded = pl.cdiv(width + 2 * experts, 128) * 128
+    spans = pl.cdiv(width, SPAN)
+    vmem = pl.BlockSpec(memory_space=pltpu.VMEM)
+    hbm = pl.BlockSpec(memory_space=pl.ANY)
+    bf16 = jnp.bfloat16
+    dma = pltpu.SemaphoreType.DMA
+
+    def body(*refs):
+        attention_kernel(experts, *refs)
+
+    return pl.pallas_call(
+        body,
+        out_shape=(
+            jax.ShapeDtypeStruct((tokens, padded), bf16),
+            jax.ShapeDtypeStruct((tokens, width), jnp.float32),
+        ),
+        in_specs=[vmem] * 8 + [hbm] * 3,
+        out_specs=(vmem, vmem),
+        scratch_shapes=[
+            pltpu.VMEM(cache_keys.shape, bf16),
+            pltpu.VMEM(cache_values.shape, bf16),
+            pltpu.VMEM((width, out_proj.shape[0]), bf16),
+            pltpu.VMEM(query.shape, bf16),
+            pltpu.VMEM((spans, tokens, SPAN), jnp.float32),
+            pltpu.VMEM((spans, tokens, SPAN), jnp.float32),
+            pltpu.VMEM((128, width), jnp.float32),
+            dma((requests // STEP,)),
+            dma((requests // STEP,)),
+            dma,
+            dma((spans,)),
+            dma((spans,)),
+        ],
+        compiler_params=pltpu.CompilerParams(
+            collective_id=1, has_side_effects=True, vmem_limit_bytes=62 * 1024 * 1024
+        ),
+    )(
+        query,
+        new_key,
+        new_value,
+        lengths[:, None],
+        residual,
+        gain[None, :],
+        router.T,
+        routes,
+        cache_keys,
+        cache_values,
+        out_proj.T,
+    )
 
 
 def per_device(
@@ -415,28 +629,18 @@
     w_up,
     w_down,
 ):
-    attended = attend(query, new_key, new_value, cache_keys, cache_values, lengths)
-    summed = lax.psum_scatter(
-        jnp.dot(attended, out_proj, preferred_element_type=jnp.float32),
-        "exp",
-        scatter_dimension=0,
-        tiled=True,
-    )
-    hidden_state = residual.astype(jnp.float32) + summed
-    mean_square = jnp.mean(hidden_state * hidden_state, axis=-1, keepdims=True)
-    normed = (hidden_state * lax.rsqrt(mean_square + 1e-05) * norm_gain).astype(jnp.bfloat16)
-    logits = jnp.dot(normed.astype(jnp.float32), router, precision=lax.Precision.HIGHEST)
-    experts = lax.axis_size("att")
-    named = jnp.any(routes[:, :, None] == jnp.arange(experts)[None, None, :], axis=1)
-    squashed = jnp.where(named, jax.nn.sigmoid(logits), 0.0)
-    gate_weights = squashed / jnp.sum(squashed, axis=1, keepdims=True)
-    coarse = lax.reduce_precision(gate_weights, 8, 7)
-    fine = (gate_weights - coarse).astype(jnp.bfloat16)
-    width = normed.shape[1]
-    spare = pl.cdiv(width + 2 * experts, 128) * 128 - width - 2 * experts
-    rows = jnp.concatenate(
-        [normed, coarse.astype(jnp.bfloat16), fine, jnp.zeros((normed.shape[0], spare), jnp.bfloat16)],
-        axis=1,
+    rows, hidden_state = attention_layer(
+        query,
+        new_key,
+        new_value,
+        cache_keys,
+        cache_values,
+        lengths,
+        out_proj,
+        residual,
+        norm_gain,
+        router,
+        routes,
     )
     return routed_experts(rows, hidden_state, w_gate, w_up, w_down)
 

time: 156 us -> 113 us (0.72)
  local copies, waits for them, and re-layouts: 41.9 us -> 5.83 us
  Pallas kernels: 81.4 us -> 107 us
  matrix products: 14.9 us -> 0 us
  between operations: 13.6 us -> 0.02 us
  other arithmetic: 3.23 us -> 0 us
    unnamed x18 -> x2, local copies, waits for them, and re-layouts: 24.4 us -> 3.13 us
    pallas_call x0 -> x1, Pallas kernels: none -> 19 us  [attention_layer(): pl.pallas_call(body, out_shape=(jax.ShapeDtypeStruct((tokens, padded), bf...]
    dot_general x4 -> x0, matrix products: 14.9 us -> none  [the longest x1 6.02 us: per_device(): jnp.dot(attended, out_proj, preferred_element_type=jnp.float32)]
    reshape x3 -> x0, local copies, waits for them, and re-layouts: 14.2 us -> none  [the longest x1 6.47 us: attend(): cached_k = cache_keys.reshape(requests, cache_len, value_heads, HEAD)]
    pallas_call x1, Pallas kernels: 81.4 us -> 88 us  [routed_experts(): pl.pallas_call(body, out_shape=jax.ShapeDtypeStruct((tokens, width), bf16...]
    broadcast_in_dim x1 -> x2, local copies, waits for them, and re-layouts: 0.01 us -> 2.7 us  [the longest x1 1.39 us: attention_layer(): lengths[:, None]]
    reduce_sum x2 -> x0, other arithmetic: 2.1 us -> none  [the longest x1 1.33 us: per_device(): mean_square = jnp.mean(hidden_state * hidden_state, axis=-1, keepdims=True)]
  transfers between devices with their start and end apart: 1 -> 0, of which waited for: 0 -> 0; matrix products, arithmetic and copies ran while one was open for 9% -> 0% of each run, Pallas kernels for 0% -> 0%
where the time goes in v2:
time: 113 us
  Pallas kernels  107 us (95%)
  local copies, waits for them, and re-layouts  5.83 us (5%)
    pallas_call x1, Pallas kernels, routed_experts(): pl.pallas_call(body, out_shape=jax.ShapeDtypeStruct((tokens, width), bf16...  88 us
    pallas_call x1, Pallas kernels, attention_layer(): pl.pallas_call(body, out_shape=(jax.ShapeDtypeStruct((tokens, padded), bf...  19 us
    unnamed x2, local copies, waits for them, and re-layouts  3.13 us

profile of v2, /device:TPU:0, one launch (start us, length us, event | category | flops | bytes accessed | tf_op | source)
XLA Modules:
  0.0 112.8 jit_solution(16278340739139588454)
XLA Ops:
  0.0 1.3 %broadcast_in_dim.7.refs_5_ = f32[1,2880]{1,0:T(1,128)} reshape(f32[2880]{0:T(1024)} %param.22) | data formatting | bytes 23040 | tf_op jit(solution)/shard_map/broadcast_in_dim | solution.py:607
  1.3 1.4 %copy.16.refs_7_ = s32[64,4]{1,0:T(8,128)} copy(s32[64,4]{0,1:T(4,128)} %param.24) | data formatting | bytes 2048 | tf_op args[10]
  2.7 1.4 %copy.15.refs_3_ = s32[128,1]{1,0:T(8,128)} copy(s32[128,1]{0,1:T(1,128)} %bitcast.9) | data formatting | bytes 1024 | tf_op jit(solution)/shard_map/broadcast_in_dim | solution.py:605
  4.1 19.0 %shard_map.136 = (bf16[64,2944]{1,0:T(8,128)(2,1)}, f32[64,2880]{1,0:T(8,128)}) custom-call(bf16[128,1024]{1,0:T(8,128)(2,1)} %refs_0_.1, bf16[128,128]{1,0:T(8,128)(2,1)} %refs_1_.1, bf16[128,128]{1,0:T(8,128)(2,1)} %refs_2_.1, s32[128,1]{1,0:T(8,128)} %copy.15.refs_3_, bf16[64,2880]{1,0:T(8,128)(2,1)} %refs_4_.2, f32[1,2880]{1,0:T(1,128)} %broadcast_in_dim.7.refs_5_, ...), custom_call_target="tpu_custom_call" | custom-call | tf_op jit(solution)/shard_map/pallas_call | solution.py:576
  23.1 88.0 %shard_map.137 = bf16[64,2880]{1,0:T(8,128)(2,1)} custom-call(bf16[64,2944]{1,0:T(8,128)(2,1)} %get-tuple-element.7.refs_0_, f32[64,2880]{1,0:T(8,128)} %get-tuple-element.8.refs_1_, bf16[1,720,2880]{2,1,0:T(8,128)(2,1)} %bitcast.6, bf16[1,720,2880]{2,1,0:T(8,128)(2,1)} %bitcast.7, bf16[1,720,2880]{2,1,0:T(8,128)(2,1)} %refs_4_.3), custom_call_target="tpu_custom_call" | custom-call | tf_op jit(solution)/shard_map/pallas_call | solution.py:337
  111.1 1.8 %copy.18 = bf16[64,2880]{1,0:T(8,128)(2,1)} copy(bf16[64,2880]{1,0:T(8,128)(2,1)} %shard_map.137) | data formatting | bytes 737280

commit v3 on v2

--- a/solution.py
+++ b/solution.py
@@ -9,6 +9,7 @@
 
 HEAD = 64
 INNER = 2
+CHUNKS = 2
 
 
 def dot_t(left, right):
@@ -51,6 +52,7 @@
     experts = rows_buf.shape[0]
     tokens = x_ref.shape[0]
     padded = x_ref.shape[1]
+    slab = tokens // CHUNKS
 
     def chip(at_line, at_side):
         return at_line * INNER + at_side
@@ -87,22 +89,25 @@
     own_copy.wait()
     pl.semaphore_wait(barrier, 2 + has_up.astype(jnp.int32) + has_down.astype(jnp.int32))
 
-    def rows_copy(block, kind, target):
+    def rows_of(chunk):
+        return pl.ds(pl.multiple_of(chunk * slab, slab), slab)
+
+    def rows_copy(block, chunk, kind, target):
         return pltpu.make_async_remote_copy(
-            src_ref=rows_buf.at[block, core],
-            dst_ref=rows_buf.at[block, core],
-            send_sem=rows_send.at[block, kind],
-            recv_sem=rows_recv.at[block, core],
+            src_ref=rows_buf.at[block, core, rows_of(chunk)],
+            dst_ref=rows_buf.at[block, core, rows_of(chunk)],
+            send_sem=rows_send.at[block, chunk, kind],
+            recv_sem=rows_recv.at[block, chunk, core],
             device_id=target,
             device_id_type=mesh_ids,
         )
 
-    def rows_arrived(block, lane):
+    def rows_arrived(block, chunk, lane):
         pltpu.make_async_remote_copy(
-            src_ref=rows_buf.at[block, lane],
-            dst_ref=rows_buf.at[block, lane],
-            send_sem=rows_send.at[block, 0],
-            recv_sem=rows_recv.at[block, lane],
+            src_ref=rows_buf.at[block, lane, rows_of(chunk)],
+            dst_ref=rows_buf.at[block, lane, rows_of(chunk)],
+            send_sem=rows_send.at[block, chunk, 0],
+            recv_sem=rows_recv.at[block, chunk, lane],
             device_id=mate_id,
             device_id_type=mesh_ids,
         ).wait_recv()
@@ -117,22 +122,22 @@
             device_id_type=mesh_ids,
         )
 
-    def side_copy(at_line):
+    def side_copy(at_line, chunk):
         return pltpu.make_async_remote_copy(
-            src_ref=part_buf.at[chip(at_line, 1 - side), core],
-            dst_ref=side_buf.at[at_line],
-            send_sem=side_send.at[at_line],
-            recv_sem=side_recv.at[at_line],
+            src_ref=part_buf.at[chip(at_line, 1 - side), core, rows_of(chunk)],
+            dst_ref=side_buf.at[at_line, rows_of(chunk)],
+            send_sem=side_send.at[at_line, chunk],
+            recv_sem=side_recv.at[at_line, chunk],
             device_id=side_id,
             device_id_type=mesh_ids,
         )
 
-    def line_copy(at_line, way, target):
+    def line_copy(at_line, chunk, way, target):
         return pltpu.make_async_remote_copy(
-            src_ref=part_buf.at[chip(at_line, side), core],
-            dst_ref=line_buf.at[way, at_line],
-            send_sem=line_send.at[at_line],
-            recv_sem=line_recv.at[way, at_line],
+            src_ref=part_buf.at[chip(at_line, side), core, rows_of(chunk)],
+            dst_ref=line_buf.at[way, at_line, rows_of(chunk)],
+            send_sem=line_send.at[at_line, chunk],
+            recv_sem=line_recv.at[way, at_line, chunk],
             device_id=target,
             device_id_type=mesh_ids,
         )
@@ -159,7 +164,61 @@
         part_buf[block] = result.reshape(2, tokens, width)
         mate_copy(block).start()
 
-    def gather_step(step, carry):
+    def compute(step, mine):
+        def one(way, carry):
+            at_line, exists = place(step, way)
+            block = chip(at_line, jnp.where(mine, side, 1 - side))
+
+            @pl.when(exists)
+            def _():
+                for chunk in range(CHUNKS):
+                    rows_arrived(block, chunk, other)
+                expert(block)
+
+            return carry
+
+        lax.fori_loop(0, 2, one, 0)
+
+    def side_sum(step):
+        def one(way, carry):
+            at_line, exists = place(step, way)
+            block = chip(at_line, 1 - side)
+
+            @pl.when(exists)
+            def _():
+                mate_copy(block).wait_recv()
+
+                def part(chunk, inner):
+                    span = rows_of(chunk)
+                    total = part_buf[block, core, span].astype(jnp.float32)
+                    total = total + mate_buf[block, span].astype(jnp.float32)
+                    part_buf[block, core, span] = total.astype(jnp.bfloat16)
+                    side_copy(at_line, chunk).start()
+                    return inner
+
+                lax.fori_loop(0, CHUNKS, part, 0)
+
+            return carry
+
+        lax.fori_loop(0, 2, one, 0)
+
+    early = max(depth - 2, 0)
+
+    def gather_step(index, carry):
+        step = index // CHUNKS
+        chunk = index % CHUNKS
+
+        @pl.when(index == CHUNKS)
+        def _():
+            for load in loads:
+                load.wait()
+
+        @pl.when(index == (depth + 1) * CHUNKS + 1)
+        def _():
+            side_sum(early)
+
+        compute(jnp.where(chunk == 0, step - 1, step - 2), chunk == 0)
+
         def relay_line(way, inner):
             at_line, exists = place(step, way)
             block = chip(at_line, side)
@@ -168,18 +227,18 @@
             def _():
                 @pl.when(step > 0)
                 def _():
-                    rows_arrived(block, core)
+                    rows_arrived(block, chunk, core)
 
                 @pl.when(has_up & (at_line <= line))
                 def _():
-                    rows_copy(block, 2, up_id).start()
+                    rows_copy(block, chunk, 2, up_id).start()
 
                 @pl.when(has_down & (at_line >= line))
                 def _():
-                    rows_copy(block, 3, down_id).start()
-
-                rows_copy(block, 1, side_id).start()
-                rows_copy(block, 0, mate_id).start()
+                    rows_copy(block, chunk, 3, down_id).start()
+
+                rows_copy(block, chunk, 1, side_id).start()
+                rows_copy(block, chunk, 0, mate_id).start()
 
             return inner
 
@@ -189,64 +248,42 @@
 
             @pl.when(exists)
             def _():
-                rows_arrived(block, core)
-                rows_copy(block, 0, mate_id).start()
+                rows_arrived(block, chunk, core)
+                rows_copy(block, chunk, 0, mate_id).start()
 
             return inner
 
         lax.fori_loop(0, 2, relay_line, 0)
         lax.fori_loop(0, 2, relay_side, 0)
-
-        @pl.when(step == 0)
+        return carry
+
+    lax.fori_loop(0, (depth + 2) * CHUNKS, gather_step, 0)
+
+    def side_step(index, carry):
+        step = depth - 1 - index
+
+        @pl.when(step != early)
         def _():
-            for load in loads:
-                load.wait()
-
-        def compute(index, inner):
-            way = index % 2
-            mine = index // 2
-            at_line, exists = place(step - mine, way)
-            block = chip(at_line, jnp.where(mine == 0, side, 1 - side))
-
-            @pl.when(exists)
-            def _():
-                rows_arrived(block, other)
-                expert(block)
-
-            return inner
-
-        lax.fori_loop(0, 4, compute, 0)
+            side_sum(step)
+
         return carry
 
-    lax.fori_loop(0, depth + 1, gather_step, 0)
-
-    def side_step(index, carry):
-        step = depth - 1 - index // 2
-        at_line, exists = place(step, index % 2)
-        block = chip(at_line, 1 - side)
-
-        @pl.when(exists)
-        def _():
-            mate_copy(block).wait_recv()
-            total = part_buf[block, core].astype(jnp.float32) + mate_buf[block].astype(jnp.float32)
-            part_buf[block, core] = total.astype(jnp.bfloat16)
-            side_copy(at_line).start()
-
-        return carry
-
-    lax.fori_loop(0, 2 * depth, side_step, 0)
-
-    def line_total(at_line):
+    lax.fori_loop(0, depth, side_step, 0)
+
+    def line_total(at_line, chunk):
         block = chip(at_line, side)
-        mate_copy(block).wait_recv()
-        side_copy(at_line).wait_recv()
-        total = part_buf[block, core].astype(jnp.float32) + mate_buf[block].astype(jnp.float32)
-        return total + side_buf[at_line].astype(jnp.float32)
+        span = rows_of(chunk)
+        side_copy(at_line, chunk).wait_recv()
+        total = part_buf[block, core, span].astype(jnp.float32)
+        total = total + mate_buf[block, span].astype(jnp.float32)
+        return total + side_buf[at_line, span].astype(jnp.float32)
 
     def line_step(index, carry):
-        step = depth - 1 - index // 2
+        step = depth - 1 - index // (2 * CHUNKS)
+        chunk = index // 2 % CHUNKS
         at_line, exists = place(step, index % 2)
         block = chip(at_line, side)
+        span = rows_of(chunk)
 
         @pl.when(exists)
         def _():
@@ -254,63 +291,73 @@
             way = jnp.where(upward, 0, 1)
             feeds = jnp.where(upward, has_down, has_up)
 
-            part_buf[block, core] = line_total(at_line).astype(jnp.bfloat16)
+            @pl.when(chunk == 0)
+            def _():
+                mate_copy(block).wait_recv()
+
+            part_buf[block, core, span] = line_total(at_line, chunk).astype(jnp.bfloat16)
 
             @pl.when(feeds)
             def _():
-                line_copy(at_line, way, up_id).wait_recv()
-                total = part_buf[block, core].astype(jnp.float32)
-                total = total + line_buf[way, at_line].astype(jnp.float32)
-                part_buf[block, core] = total.astype(jnp.bfloat16)
+                line_copy(at_line, chunk, way, up_id).wait_recv()
+                total = part_buf[block, core, span].astype(jnp.float32)
+                total = total + line_buf[way, at_line, span].astype(jnp.float32)
+                part_buf[block, core, span] = total.astype(jnp.bfloat16)
 
             @pl.when(upward)
             def _():
-                line_copy(at_line, 0, up_id).start()
+                line_copy(at_line, chunk, 0, up_id).start()
 
             @pl.when(jnp.logical_not(upward))
             def _():
-                line_copy(at_line, 1, down_id).start()
+                line_copy(at_line, chunk, 1, down_id).start()
 
         return carry
 
-    lax.fori_loop(0, 2 * (depth - 1), line_step, 0)
-
-    hidden_ref[...] = hidden_ref[...] + line_total(line)
-
-    @pl.when(has_down)
-    def _():
-        line_copy(line, 0, up_id).wait_recv()
-        hidden_ref[...] = hidden_ref[...] + line_buf[0, line].astype(jnp.float32)
-
-    @pl.when(has_up)
-    def _():
-        line_copy(line, 1, up_id).wait_recv()
-        hidden_ref[...] = hidden_ref[...] + line_buf[1, line].astype(jnp.float32)
-
-    out_ref[...] = hidden_ref[...].astype(out_ref.dtype)
+    lax.fori_loop(0, 2 * CHUNKS * (depth - 1), line_step, 0)
+
+    mate_copy(me).wait_recv()
+
+    def finish(chunk, carry):
+        span = rows_of(chunk)
+        for exists, way in ((has_down, 0), (has_up, 1)):
+
+            @pl.when(exists)
+            def _():
+                line_copy(line, chunk, way, up_id).wait_recv()
+                hidden_ref[span, :] = hidden_ref[span, :] + line_buf[way, line, span].astype(
+                    jnp.float32
+                )
+
+        total = hidden_ref[span, :] + line_total(line, chunk)
+        out_ref[span, :] = total.astype(out_ref.dtype)
+        return carry
+
+    lax.fori_loop(0, CHUNKS, finish, 0)
 
     def drain(at_line, carry):
         block = chip(at_line, side)
         across = chip(at_line, 1 - side)
-        rows_copy(block, 0, mate_id).wait_send()
-        rows_copy(block, 1, side_id).wait_send()
-        rows_copy(across, 0, mate_id).wait_send()
-
-        @pl.when(has_up & (at_line <= line))
-        def _():
-            rows_copy(block, 2, up_id).wait_send()
-
-        @pl.when(has_down & (at_line >= line))
-        def _():
-            rows_copy(block, 3, down_id).wait_send()
-
         mate_copy(block).wait_send()
         mate_copy(across).wait_send()
-        side_copy(at_line).wait_send()
-
-        @pl.when(at_line != line)
-        def _():
-            line_copy(at_line, 0, up_id).wait_send()
+        for chunk in range(CHUNKS):
+            rows_copy(block, chunk, 0, mate_id).wait_send()
+            rows_copy(block, chunk, 1, side_id).wait_send()
+            rows_copy(across, chunk, 0, mate_id).wait_send()
+
+            @pl.when(has_up & (at_line <= line))
+            def _():
+                rows_copy(block, chunk, 2, up_id).wait_send()
+
+            @pl.when(has_down & (at_line >= line))
+            def _():
+                rows_copy(block, chunk, 3, down_id).wait_send()
+
+            side_copy(at_line, chunk).wait_send()
+
+            @pl.when(at_line != line)
+            def _():
+                line_copy(at_line, chunk, 0, up_id).wait_send()
 
         return carry
 
@@ -350,14 +397,14 @@
             pltpu.VMEM((inner, width), bf16),
             dma((3,)),
             dma,
-            dma((experts, 4)),
-            dma((experts, 2)),
+            dma((experts, CHUNKS, 4)),
+            dma((experts, CHUNKS, 2)),
             dma((experts,)),
             dma((experts,)),
-            dma((depth,)),
-            dma((depth,)),
-            dma((depth,)),
-            dma((2, depth)),
+            dma((depth, CHUNKS)),
+            dma((depth, CHUNKS)),
+            dma((depth, CHUNKS)),
+            dma((2, depth, CHUNKS)),
             pltpu.VMEM((tokens, width), jnp.float32),
         ],
         compiler_params=pltpu.CompilerParams(
@@ -386,12 +433,15 @@
     stacked = jnp.concatenate(pieces, axis=0)
     tall_key = jnp.concatenate([new_key] * heads, axis=0)
     tall_value = jnp.concatenate([new_value] * heads, axis=0)
-    tall_length = jnp.concatenate([lengths] * heads, axis=0)
     fresh = jnp.sum(stacked * tall_key, axis=1, keepdims=True) * inverse_root
     scores = dot_t(stacked.astype(jnp.bfloat16), keys.reshape(rows * cache_len, pair)) * inverse_root
     position = lax.broadcasted_iota(jnp.int32, scores.shape, 1)
     row = lax.broadcasted_iota(jnp.int32, (scores.shape[0], 1), 0)
-    start = (row % rows) * cache_len
+    request = row % rows
+    start = request * cache_len
+    tall_length = jnp.zeros_like(row)
+    for at in range(rows):
+        tall_length = jnp.where(request == at, lengths[at], tall_length)
     live = (position >= start) & (position < start + tall_length)
     scores = jnp.where(live, scores, -1e30)
     highest = jnp.maximum(jnp.max(scores, axis=1, keepdims=True), fresh)
@@ -484,15 +534,15 @@
         query = query_ref[span, :].astype(jnp.float32)
         new_key = new_key_ref[span, :].astype(jnp.float32)
         new_value = new_value_ref[span, :].astype(jnp.float32)
-        lengths = lengths_ref[span, :]
         keys = keys_buf[span]
         values = values_buf[span]
         parts = []
         for half in range(STEP // HALF):
             cut = slice(half * HALF, (half + 1) * HALF)
+            lengths = [lengths_ref[step * STEP + half * HALF + at] for at in range(HALF)]
             parts.append(
                 attend_block(
-                    query[cut], new_key[cut], new_value[cut], keys[cut], values[cut], lengths[cut]
+                    query[cut], new_key[cut], new_value[cut], keys[cut], values[cut], lengths
                 )
             )
         attended[span, :] = jnp.concatenate(parts, axis=0).astype(jnp.bfloat16)
@@ -531,7 +581,7 @@
         hidden_ref[:, begin:end] = total
         squares = squares + jnp.sum(total * total, axis=1, keepdims=True)
     scale = lax.rsqrt(squares / width + 1e-05)
-    normed = (hidden_ref[...] * scale * gain_ref[...]).astype(jnp.bfloat16)
+    normed = (hidden_ref[...] * scale * gain_ref[...].reshape(1, width)).astype(jnp.bfloat16)
     logits = lax.dot_general(
         normed.astype(jnp.float32),
         wide_router[...],
@@ -542,10 +592,12 @@
     lane = lax.broadcasted_iota(jnp.int32, logits.shape, 1) - base
     coarse_lane = (lane >= 0) & (lane < experts)
     fine_lane = (lane >= experts) & (lane < 2 * experts)
-    expert = jnp.where(fine_lane, lane - experts, lane)
-    named = jnp.zeros(logits.shape, jnp.bool_)
-    for at in range(routes_ref.shape[1]):
-        named = named | (routes_ref[:, at : at + 1] == expert)
+    column = lax.broadcasted_iota(jnp.int32, (logits.shape[1], 1), 0) - base
+    column = jnp.where(column >= experts, column - experts, column)
+    hits = jnp.zeros((logits.shape[1], tokens), jnp.float32)
+    for at in range(routes_ref.shape[0]):
+        hits = jnp.where(routes_ref[at : at + 1, :] == column, 1.0, hits)
+    named = hits.T > 0.5
     squashed = jnp.where(named, 1.0 / (1.0 + jnp.exp(-logits)), 0.0)
     totals = jnp.sum(jnp.where(coarse_lane, squashed, 0.0), axis=1, keepdims=True)
     weight = squashed / totals
@@ -579,7 +631,7 @@
             jax.ShapeDtypeStruct((tokens, padded), bf16),
             jax.ShapeDtypeStruct((tokens, width), jnp.float32),
         ),
-        in_specs=[vmem] * 8 + [hbm] * 3,
+        in_specs=[vmem] * 3 + [pl.BlockSpec(memory_space=pltpu.SMEM)] + [vmem] * 4 + [hbm] * 3,
         out_specs=(vmem, vmem),
         scratch_shapes=[
             pltpu.VMEM(cache_keys.shape, bf16),
@@ -602,11 +654,11 @@
         query,
         new_key,
         new_value,
-        lengths[:, None],
+        lengths,
         residual,
-        gain[None, :],
+        gain,
         router.T,
-        routes,
+        routes.T,
         cache_keys,
         cache_values,
         out_proj.T,

time: 113 us -> 104 us (0.920)
  Pallas kernels: 107 us -> 102 us
  local copies, waits for them, and re-layouts: 5.83 us -> 1.76 us
    pallas_call x1, Pallas kernels: 88 us -> 82.9 us  [routed_experts(): pl.pallas_call(body, out_shape=jax.ShapeDtypeStruct((tokens, width), bf16...]
    broadcast_in_dim x2 -> x0, local copies, waits for them, and re-layouts: 2.7 us -> none  [the longest x1 1.39 us: attention_layer(): lengths[:, None]]
    unnamed x2 -> x1, local copies, waits for them, and re-layouts: 3.13 us -> 1.76 us
where the time goes in v3:
time: 104 us
  Pallas kernels  102 us (98%)
  local copies, waits for them, and re-layouts  1.76 us (2%)
    pallas_call x1, Pallas kernels, routed_experts(): pl.pallas_call(body, out_shape=jax.ShapeDtypeStruct((tokens, width), bf16...  82.9 us
    pallas_call x1, Pallas kernels, attention_layer(): pl.pallas_call(body, out_shape=(jax.ShapeDtypeStruct((tokens, padded), bf...  19.1 us

profile of v3, /device:TPU:0, one launch (start us, length us, event | category | flops | bytes accessed | tf_op | source)
XLA Modules:
  0.0 103.8 jit_solution(17466806717177340752)
XLA Ops:
  0.0 19.1 %shard_map.136 = (bf16[64,2944]{1,0:T(8,128)(2,1)}, f32[64,2880]{1,0:T(8,128)}) custom-call(bf16[128,1024]{1,0:T(8,128)(2,1)} %refs_0_.1, bf16[128,128]{1,0:T(8,128)(2,1)} %refs_1_.1, bf16[128,128]{1,0:T(8,128)(2,1)} %refs_2_.1, s32[128]{0:T(128)} %refs_3_.1, bf16[64,2880]{1,0:T(8,128)(2,1)} %refs_4_.2, f32[2880]{0:T(1024)} %refs_5_.1, f32[8,2880]{1,0:T(8,128)} %bitcast.8, ...), custom_call_target="tpu_custom_call" | custom-call | tf_op jit(solution)/shard_map/pallas_call | solution.py:628
  19.1 82.9 %shard_map.137 = bf16[64,2880]{1,0:T(8,128)(2,1)} custom-call(bf16[64,2944]{1,0:T(8,128)(2,1)} %get-tuple-element.7.refs_0_, f32[64,2880]{1,0:T(8,128)} %get-tuple-element.8.refs_1_, bf16[1,720,2880]{2,1,0:T(8,128)(2,1)} %bitcast.6, bf16[1,720,2880]{2,1,0:T(8,128)(2,1)} %bitcast.7, bf16[1,720,2880]{2,1,0:T(8,128)(2,1)} %refs_4_.3), custom_call_target="tpu_custom_call" | custom-call | tf_op jit(solution)/shard_map/pallas_call | solution.py:384
  102.1 1.8 %copy.16 = bf16[64,2880]{1,0:T(8,128)(2,1)} copy(bf16[64,2880]{1,0:T(8,128)(2,1)} %shard_map.137) | data formatting | bytes 737280

commit v4 on v3

--- a/solution.py
+++ b/solution.py
@@ -42,6 +42,9 @@
     side_recv,
     line_send,
     line_recv,
+    far_buf,
+    far_send,
+    far_recv,
 ):
     me = lax.axis_index("att")
     core = lax.axis_index("exp")
@@ -89,6 +92,9 @@
     own_copy.wait()
     pl.semaphore_wait(barrier, 2 + has_up.astype(jnp.int32) + has_down.astype(jnp.int32))
 
+    def crosses_first(at_line, chunk):
+        return ((at_line == 0) | (at_line == depth - 1)) & (chunk == CHUNKS - 1)
+
     def rows_of(chunk):
         return pl.ds(pl.multiple_of(chunk * slab, slab), slab)
 
@@ -131,6 +137,24 @@
             device_id=side_id,
             device_id_type=mesh_ids,
         )
+
+    def far_copy(at_line, way, target):
+        return pltpu.make_async_remote_copy(
+            src_ref=part_buf.at[chip(at_line, 1 - side), core, rows_of(CHUNKS - 1)],
+            dst_ref=far_buf.at[way],
+            send_sem=far_send.at[way],
+            recv_sem=far_recv.at[way],
+            device_id=target,
+            device_id_type=mesh_ids,
+        )
+
+    def far_add(at_line, way):
+        far_copy(at_line, way, up_id).wait_recv()
+        across = chip(at_line, 1 - side)
+        span = rows_of(CHUNKS - 1)
+        total = part_buf[across, core, span].astype(jnp.float32)
+        total = total + far_buf[way].astype(jnp.float32)
+        part_buf[across, core, span] = total.astype(jnp.bfloat16)
 
     def line_copy(at_line, chunk, way, target):
         return pltpu.make_async_remote_copy(
@@ -193,7 +217,11 @@
                     total = part_buf[block, core, span].astype(jnp.float32)
                     total = total + mate_buf[block, span].astype(jnp.float32)
                     part_buf[block, core, span] = total.astype(jnp.bfloat16)
-                    side_copy(at_line, chunk).start()
+
+                    @pl.when(jnp.logical_not(crosses_first(at_line, chunk)))
+                    def _():
+                        side_copy(at_line, chunk).start()
+
                     return inner
 
                 lax.fori_loop(0, CHUNKS, part, 0)
@@ -237,7 +265,10 @@
                 def _():
                     rows_copy(block, chunk, 3, down_id).start()
 
-                rows_copy(block, chunk, 1, side_id).start()
+                @pl.when((step == 0) | jnp.logical_not(crosses_first(at_line, chunk)))
+                def _():
+                    rows_copy(block, chunk, 1, side_id).start()
+
                 rows_copy(block, chunk, 0, mate_id).start()
 
             return inner
@@ -249,6 +280,16 @@
             @pl.when(exists)
             def _():
                 rows_arrived(block, chunk, core)
+                crossed = crosses_first(at_line, chunk)
+
+                @pl.when(crossed & has_up & (at_line <= line))
+                def _():
+                    rows_copy(block, chunk, 2, up_id).start()
+
+                @pl.when(crossed & has_down & (at_line >= line))
+                def _():
+                    rows_copy(block, chunk, 3, down_id).start()
+
                 rows_copy(block, chunk, 0, mate_id).start()
 
             return inner
@@ -270,17 +311,19 @@
 
     lax.fori_loop(0, depth, side_step, 0)
 
-    def line_total(at_line, chunk):
+    def mate_total(at_line, chunk):
         block = chip(at_line, side)
         span = rows_of(chunk)
+        total = part_buf[block, core, span].astype(jnp.float32)
+        return total + mate_buf[block, span].astype(jnp.float32)
+
+    def line_total(at_line, chunk):
         side_copy(at_line, chunk).wait_recv()
-        total = part_buf[block, core, span].astype(jnp.float32)
-        total = total + mate_buf[block, span].astype(jnp.float32)
-        return total + side_buf[at_line, span].astype(jnp.float32)
+        return mate_total(at_line, chunk) + side_buf[at_line, rows_of(chunk)].astype(jnp.float32)
 
     def line_step(index, carry):
         step = depth - 1 - index // (2 * CHUNKS)
-        chunk = index // 2 % CHUNKS
+        chunk = CHUNKS - 1 - index // 2 % CHUNKS
         at_line, exists = place(step, index % 2)
         block = chip(at_line, side)
         span = rows_of(chunk)
@@ -291,11 +334,31 @@
             way = jnp.where(upward, 0, 1)
             feeds = jnp.where(upward, has_down, has_up)
 
-            @pl.when(chunk == 0)
+            crossed = crosses_first(at_line, chunk)
+
+            @pl.when(chunk == CHUNKS - 1)
             def _():
                 mate_copy(block).wait_recv()
 
-            part_buf[block, core, span] = line_total(at_line, chunk).astype(jnp.bfloat16)
+            @pl.when(crossed & feeds)
+            def _():
+                far_add(at_line, way)
+
+            @pl.when(crossed & upward)
+            def _():
+                far_copy(at_line, 0, up_id).start()
+
+            @pl.when(crossed & jnp.logical_not(upward))
+            def _():
+                far_copy(at_line, 1, down_id).start()
+
+            @pl.when(crossed)
+            def _():
+                part_buf[block, core, span] = mate_total(at_line, chunk).astype(jnp.bfloat16)
+
+            @pl.when(jnp.logical_not(crossed))
+            def _():
+                part_buf[block, core, span] = line_total(at_line, chunk).astype(jnp.bfloat16)
 
             @pl.when(feeds)
             def _():
@@ -317,6 +380,13 @@
     lax.fori_loop(0, 2 * CHUNKS * (depth - 1), line_step, 0)
 
     mate_copy(me).wait_recv()
+
+    for at_end, way in ((line == 0, 1), (line == depth - 1, 0)):
+
+        @pl.when(at_end)
+        def _():
+            far_add(line, way)
+            side_copy(line, CHUNKS - 1).start()
 
     def finish(chunk, carry):
         span = rows_of(chunk)
@@ -342,9 +412,27 @@
         mate_copy(across).wait_send()
         for chunk in range(CHUNKS):
             rows_copy(block, chunk, 0, mate_id).wait_send()
-            rows_copy(block, chunk, 1, side_id).wait_send()
+            crossed = crosses_first(at_line, chunk)
+
+            @pl.when(jnp.logical_not(crossed) | (at_line == line))
+            def _():
+                rows_copy(block, chunk, 1, side_id).wait_send()
+                side_copy(at_line, chunk).wait_send()
+
             rows_copy(across, chunk, 0, mate_id).wait_send()
 
+            @pl.when(crossed & has_up & (at_line <= line))
+            def _():
+                rows_copy(across, chunk, 2, up_id).wait_send()
+
+            @pl.when(crossed & has_down & (at_line >= line))
+            def _():
+                rows_copy(across, chunk, 3, down_id).wait_send()
+
+            @pl.when(crossed & (at_line != line))
+            def _():
+                far_copy(at_line, jnp.where(at_line == 0, 1, 0), up_id).wait_send()
+
             @pl.when(has_up & (at_line <= line))
             def _():
                 rows_copy(block, chunk, 2, up_id).wait_send()
@@ -352,8 +440,6 @@
             @pl.when(has_down & (at_line >= line))
             def _():
                 rows_copy(block, chunk, 3, down_id).wait_send()
-
-            side_copy(at_line, chunk).wait_send()
 
             @pl.when(at_line != line)
             def _():
@@ -405,6 +491,9 @@
             dma((depth, CHUNKS)),
             dma((depth, CHUNKS)),
             dma((2, depth, CHUNKS)),
+            pltpu.VMEM((2, tokens // CHUNKS, width), bf16),
+            dma((2,)),
+            dma((2,)),
             pltpu.VMEM((tokens, width), jnp.float32),
         ],
         compiler_params=pltpu.CompilerParams(
@@ -582,13 +671,13 @@
         squares = squares + jnp.sum(total * total, axis=1, keepdims=True)
     scale = lax.rsqrt(squares / width + 1e-05)
     normed = (hidden_ref[...] * scale * gain_ref[...].reshape(1, width)).astype(jnp.bfloat16)
-    logits = lax.dot_general(
-        normed.astype(jnp.float32),
-        wide_router[...],
-        (((1,), (1,)), ((), ())),
-        precision=lax.Precision.HIGHEST,
-        preferred_element_type=jnp.float32,
-    )
+    pieces = []
+    rest = wide_router[...]
+    for _ in range(3):
+        piece = rest.astype(jnp.bfloat16)
+        rest = rest - piece.astype(jnp.float32)
+        pieces.append(piece)
+    logits = dot_t(normed, pieces[0]) + (dot_t(normed, pieces[1]) + dot_t(normed, pieces[2]))
     lane = lax.broadcasted_iota(jnp.int32, logits.shape, 1) - base
     coarse_lane = (lane >= 0) & (lane < experts)
     fine_lane = (lane >= experts) & (lane < 2 * experts)

time: 104 us -> 102 us (0.981)
  Pallas kernels: 102 us -> 99.2 us
    pallas_call x1, Pallas kernels: 19.1 us -> 17.1 us  [attention_layer(): pl.pallas_call(body, out_shape=(jax.ShapeDtypeStruct((tokens, padded), bf...]
where the time goes in v4:
time: 102 us; the launch traced here: 101 us
  Pallas kernels  99.2 us (97%)
  local copies, waits for them, and re-layouts  1.76 us (2%)
    pallas_call x1, Pallas kernels, routed_experts(): pl.pallas_call(body, out_shape=jax.ShapeDtypeStruct((tokens, width), bf16...  82.1 us
    pallas_call x1, Pallas kernels, attention_layer(): pl.pallas_call(body, out_shape=(jax.ShapeDtypeStruct((tokens, padded), bf...  17.1 us

profile of v4, /device:TPU:0, one launch (start us, length us, event | category | flops | bytes accessed | tf_op | source)
XLA Modules:
  0.0 101.0 jit_solution(9172933045166784471)
XLA Ops:
  0.0 17.1 %shard_map.136 = (bf16[64,2944]{1,0:T(8,128)(2,1)}, f32[64,2880]{1,0:T(8,128)}) custom-call(bf16[128,1024]{1,0:T(8,128)(2,1)} %refs_0_.1, bf16[128,128]{1,0:T(8,128)(2,1)} %refs_1_.1, bf16[128,128]{1,0:T(8,128)(2,1)} %refs_2_.1, s32[128]{0:T(128)} %refs_3_.1, bf16[64,2880]{1,0:T(8,128)(2,1)} %refs_4_.2, f32[2880]{0:T(1024)} %refs_5_.1, f32[8,2880]{1,0:T(8,128)} %bitcast.8, ...), custom_call_target="tpu_custom_call" | custom-call | tf_op jit(solution)/shard_map/pallas_call | solution.py:717
  17.2 82.1 %shard_map.137 = bf16[64,2880]{1,0:T(8,128)(2,1)} custom-call(bf16[64,2944]{1,0:T(8,128)(2,1)} %get-tuple-element.7.refs_0_, f32[64,2880]{1,0:T(8,128)} %get-tuple-element.8.refs_1_, bf16[1,720,2880]{2,1,0:T(8,128)(2,1)} %bitcast.6, bf16[1,720,2880]{2,1,0:T(8,128)(2,1)} %bitcast.7, bf16[1,720,2880]{2,1,0:T(8,128)(2,1)} %refs_4_.3), custom_call_target="tpu_custom_call" | custom-call | tf_op jit(solution)/shard_map/pallas_call | solution.py:470
  99.3 1.8 %copy.16 = bf16[64,2880]{1,0:T(8,128)(2,1)} copy(bf16[64,2880]{1,0:T(8,128)(2,1)} %shard_map.137) | data formatting | bytes 737280
